TPU v7x, 128 devices: a whole 4x4x4 slice. The times are simulated.
128 devices in a mesh: dp: 64 (over z, y, x), fsdp: 2 (over core).
Axes of the slice: x: 4, y: 4, z: 4, core: 2. Of those that a mesh axis runs over, the one named last changes fastest.
Arguments:
- mel_panels: bfloat16 [8192, 10240], P(('dp', 'fsdp')), may hold values from -6 to 6
- frames: int32 [8192], P(('dp', 'fsdp')), may hold values from 0 to 128, as said below
- target: int32 [8192], P(('dp', 'fsdp')), may hold values from 0 to 63, as said below
- conv_first: bfloat16 [9, 256], P(None, 'fsdp'), may hold values from -2 to 2
- depth_a: bfloat16 [9, 256], P(None, 'fsdp'), may hold values from -3 to 3
- point_a: bfloat16 [256, 256], P(None, 'fsdp'), may hold values from -0.5 to 0.5
- depth_b: bfloat16 [9, 256], P(None, 'fsdp'), may hold values from -3 to 3
- point_b: bfloat16 [256, 256], P(None, 'fsdp'), may hold values from -0.5 to 0.5
- linear_weight: bfloat16 [2560, 1024], P(None, 'fsdp'), may hold values from -0.15625 to 0.15625
- norm_gain: bfloat16 [1024], P('fsdp'), may hold values from 0.099609375 to 1.8984375
- up_weight: bfloat16 [1024, 2048], P(None, 'fsdp'), may hold values from -0.1875 to 0.1875
- depth_kernel: bfloat16 [9, 1024], P(None, 'fsdp'), may hold values from -2 to 2
- conv_gain: bfloat16 [1024], P('fsdp'), may hold values from 0.099609375 to 1.8984375
- down_weight: bfloat16 [1024, 1024], P('fsdp'), may hold values from -0.1875 to 0.1875
- cotangent: bfloat16 [65536, 1024], P(('dp', 'fsdp')), may hold values from -6 to 6
Outputs:
- layer_out: bfloat16 [65536, 1024], P(('dp', 'fsdp'))
- grad_input: bfloat16 [65536, 1024], P(('dp', 'fsdp'))
- grad_down: float32 [1024, 1024], P('fsdp')
Inputs may be any that keep to these rules, and one draw needn't show every extreme that they name: The slots of one loader are those of one index of dp and fsdp. A live slot holds a panel of 8 * m frames with 8 * m >= 32; frames = 0 marks an empty slot. Every device receives exactly 32 panels from the loaders of its own fsdp index, at most one from any loader, and one of them has 128 frames. `target`: only live slots are sent.
All inputs are finite; a program needn't handle non-finite values.
Results may differ from a plain program's by a relative error of at most 0.017.
Values may be sent and summed in bfloat16 or wider, within the bound.
A program may use at most 192 MiB of HBM per device.

v0:
```python
import math

import jax
import jax.numpy as jnp
from jax import lax
from jax.sharding import PartitionSpec as P

MELS = 80
PANEL = 128


EPSILON = 1e-05


def sent_together(arrays, axis, dim, along):
    widths = [a.shape[along] for a in arrays]
    both = jnp.concatenate(arrays, axis=along)
    out = lax.all_gather(both, axis, axis=dim, tiled=True)
    return tuple(jnp.split(out, [sum(widths[:k]) for k in range(1, len(widths))], axis=along))


def in_order(tiles, dim):
    dims = list(tiles.shape[1:])
    dims[dim] *= tiles.shape[0]
    return jnp.moveaxis(tiles, 0, dim).reshape(dims)


def gather_together(arrays, axis, dims):
    line = jnp.concatenate([a.reshape(-1) for a in arrays])
    lines, at, done = (lax.all_gather(line, axis), 0, [])
    for a, dim in zip(arrays, dims):
        tiles = lines[:, at : at + a.size].reshape(-1, *a.shape)
        done.append(in_order(tiles, dim))
        at += a.size
    return tuple(done)


def in_blocks(value, dim, size):
    before, after = (value.shape[:dim], value.shape[dim + 1 :])
    return jnp.moveaxis(value.reshape(*before, size, -1, *after), dim, 0)


def sent_and_summed(value, axis, dim):
    size = lax.axis_size(axis)
    tiles = lax.all_to_all(in_blocks(value, dim, size), axis, 0, 0, tiled=True)
    return jnp.sum(tiles.astype(jnp.float32), axis=0)


def phase_rows(source):
    shape_in = source.shape
    split = source.reshape((shape_in[0], shape_in[1] // 2, 2) + shape_in[2:])
    even = split[:, :, 0]
    odd = split[:, :, 1]
    before = jnp.concatenate([jnp.zeros_like(odd[:, :1]), odd[:, :-1]], axis=1)
    return (before, even, odd)


def phase_cols(source):
    shape_in = source.shape
    split = source.reshape(shape_in[:2] + (shape_in[2] // 2, 2) + shape_in[3:])
    even = split[:, :, :, 0]
    odd = split[:, :, :, 1]
    before = jnp.concatenate([jnp.zeros_like(odd[:, :, :1]), odd[:, :, :-1]], axis=2)
    return (before, even, odd)


def first_section(masked, weights):
    height = masked.shape[1] // 2
    breadth = masked.shape[2] // 2
    summed = jnp.zeros((masked.shape[0], height, breadth, weights.shape[1]), jnp.float32)
    row_views = phase_rows(masked)
    for i in range(3):
        col_views = phase_cols(row_views[i])
        for j in range(3):
            window = col_views[j].astype(jnp.float32)
            summed = summed + window[:, :, :, None] * weights[3 * i + j].astype(jnp.float32)
    return jnp.maximum(summed, 0.0).astype(jnp.bfloat16)


def depth_stride(source, weights):
    height = source.shape[1] // 2
    breadth = source.shape[2] // 2
    summed = jnp.zeros((source.shape[0], height, breadth, source.shape[3]), jnp.float32)
    row_views = phase_rows(source)
    for i in range(3):
        col_views = phase_cols(row_views[i])
        for j in range(3):
            window = col_views[j].astype(jnp.float32)
            summed = summed + window * weights[3 * i + j].astype(jnp.float32)
    return summed.astype(jnp.bfloat16)


def point_relu(spread, weights):
    shape_in = spread.shape
    mapped = jnp.dot(spread.reshape(-1, shape_in[3]), weights, preferred_element_type=jnp.float32)
    return jnp.maximum(mapped, 0.0).astype(jnp.bfloat16).reshape(shape_in[:3] + (weights.shape[1],))


def subsample(block_panels, block_lengths, conv_first, depth_a, point_a, depth_b, point_b):
    number = block_panels.shape[0]
    frames_in = block_panels.reshape(number, PANEL, MELS)
    inside = jnp.arange(PANEL)[None, :] < block_lengths[:, None]
    masked = jnp.where(inside[:, :, None], frames_in, jnp.zeros_like(frames_in))
    first = first_section(masked, conv_first)
    second = point_relu(depth_stride(first, depth_a), point_a)
    fourth = point_relu(depth_stride(second, depth_b), point_b)
    return fourth.reshape(number * fourth.shape[1], fourth.shape[2] * fourth.shape[3])


def depth_forward(gated, kernel, span):
    groups_in = gated.shape[0] // span
    half_width = kernel.shape[0] // 2
    shaped = jnp.pad(gated.reshape(groups_in, span, -1), ((0, 0), (half_width, half_width), (0, 0)))
    summed = jnp.zeros((groups_in, span, gated.shape[1]), jnp.float32)
    for k in range(kernel.shape[0]):
        summed = summed + shaped[:, k : k + span].astype(jnp.float32) * kernel[k].astype(
            jnp.float32
        )
    return summed.reshape(gated.shape[0], -1)


def depth_backward(upstream, kernel, span):
    groups_in = upstream.shape[0] // span
    half_width = kernel.shape[0] // 2
    shaped = jnp.pad(
        upstream.reshape(groups_in, span, -1), ((0, 0), (half_width, half_width), (0, 0))
    )
    summed = jnp.zeros((groups_in, span, upstream.shape[1]), jnp.float32)
    for k in range(kernel.shape[0]):
        offset = 2 * half_width - k
        summed = summed + shaped[:, offset : offset + span] * kernel[k].astype(jnp.float32)
    return summed.reshape(upstream.shape[0], -1)


def module_pass(
    features, keep, cotangent, norm_gain, up_weight, depth_kernel, conv_gain, down_weight, span
):
    width = features.shape[1]
    values = features.astype(jnp.float32)
    centred = values - jnp.mean(values, axis=1, keepdims=True)
    scale_one = lax.rsqrt(jnp.mean(centred * centred, axis=1, keepdims=True) + EPSILON)
    standard = centred * scale_one
    normed = (standard * norm_gain.astype(jnp.float32)).astype(jnp.bfloat16)
    projected = jnp.dot(normed, up_weight, preferred_element_type=jnp.float32)
    value_half = projected[:, :width]
    gate_half = jax.nn.sigmoid(projected[:, width:])
    row_keep = keep[:, None]
    gated = (row_keep * value_half * gate_half).astype(jnp.bfloat16)
    depthwise = depth_forward(gated, depth_kernel, span)
    centred_two = depthwise - jnp.mean(depthwise, axis=1, keepdims=True)
    scale_two = lax.rsqrt(jnp.mean(centred_two * centred_two, axis=1, keepdims=True) + EPSILON)
    standard_two = centred_two * scale_two
    active = standard_two * conv_gain.astype(jnp.float32)
    swish_gate = jax.nn.sigmoid(active)
    hidden = (active * swish_gate).astype(jnp.bfloat16)
    mixed = jnp.dot(hidden, down_weight, preferred_element_type=jnp.float32)
    layer_out = (row_keep * (values + mixed)).astype(jnp.bfloat16)
    back_out = jnp.where(row_keep > 0, cotangent, jnp.zeros_like(cotangent))
    back_hidden = lax.dot_general(
        back_out, down_weight, (((1,), (1,)), ((), ())), preferred_element_type=jnp.float32
    )
    back_active = back_hidden * (swish_gate + active * swish_gate * (1.0 - swish_gate))
    gain_back = back_active * conv_gain.astype(jnp.float32)
    back_depth = scale_two * (
        gain_back
        - jnp.mean(gain_back, axis=1, keepdims=True)
        - standard_two * jnp.mean(gain_back * standard_two, axis=1, keepdims=True)
    )
    back_gated = row_keep * depth_backward(back_depth, depth_kernel, span)
    back_proj = jnp.concatenate(
        [back_gated * gate_half, back_gated * value_half * gate_half * (1.0 - gate_half)], axis=1
    ).astype(jnp.bfloat16)
    back_normed = lax.dot_general(
        back_proj, up_weight, (((1,), (1,)), ((), ())), preferred_element_type=jnp.float32
    )
    gain_front = back_normed * norm_gain.astype(jnp.float32)
    back_input = scale_one * (
        gain_front
        - jnp.mean(gain_front, axis=1, keepdims=True)
        - standard * jnp.mean(gain_front * standard, axis=1, keepdims=True)
    )
    grad_input = (back_out.astype(jnp.float32) + back_input).astype(jnp.bfloat16)
    return (layer_out, grad_input, hidden, back_out)


def local(
    mel_panels,
    frames,
    target,
    conv_first,
    depth_a,
    point_a,
    depth_b,
    point_b,
    linear_weight,
    norm_gain,
    up_weight,
    depth_kernel,
    conv_gain,
    down_weight,
    cotangent,
):
    groups = lax.axis_size("dp")
    members = lax.axis_size("fsdp")
    span = PANEL // 8
    panel_count = cotangent.shape[0] // span
    destinations = jnp.arange(groups, dtype=jnp.int32)
    selected = (target[None, :] == destinations[:, None]) & (frames[None, :] > 0)
    outgoing = jnp.dot(
        selected.astype(jnp.bfloat16), mel_panels, preferred_element_type=jnp.float32
    ).astype(jnp.bfloat16)
    sent_frames = jnp.sum(jnp.where(selected, frames[None, :], 0), axis=1)
    incoming, got_frames = (
        lax.all_to_all(outgoing, "dp", split_axis=0, concat_axis=0, tiled=True),
        lax.all_to_all(sent_frames, "dp", split_axis=0, concat_axis=0, tiled=True),
    )
    present = got_frames > 0
    position = jnp.cumsum(present.astype(jnp.int32)) - 1
    places = jnp.arange(panel_count, dtype=jnp.int32)
    placing = (position[None, :] == places[:, None]) & present[None, :]
    panels = jnp.dot(
        placing.astype(jnp.bfloat16), incoming, preferred_element_type=jnp.float32
    ).astype(jnp.bfloat16)
    lengths = jnp.sum(jnp.where(placing, got_frames[None, :], 0), axis=1).astype(jnp.int32)
    first_full, depth_one, point_one, depth_two, point_two, gain_front, kernel_full, gain_back = (
        *sent_together((conv_first, depth_a, point_a, depth_b, point_b), "fsdp", 1, 0),
        lax.all_gather(norm_gain, "fsdp", axis=0, tiled=True),
        lax.all_gather(depth_kernel, "fsdp", axis=1, tiled=True),
        lax.all_gather(conv_gain, "fsdp", axis=0, tiled=True),
    )
    per_block = math.gcd(panel_count, 16)

    def sub_block(block_args):
        return subsample(
            block_args[0], block_args[1], first_full, depth_one, point_one, depth_two, point_two
        )

    flat_rows = lax.map(
        sub_block,
        (
            panels.reshape(panel_count // per_block, per_block, -1),
            lengths.reshape(panel_count // per_block, per_block),
        ),
    )
    flat_rows = flat_rows.reshape(panel_count * span, -1)
    features = jnp.dot(
        flat_rows,
        lax.all_gather(linear_weight, "fsdp", axis=1, tiled=True),
        preferred_element_type=jnp.float32,
    ).astype(jnp.bfloat16)
    keep = (jnp.arange(span)[None, :] < (lengths // 8)[:, None]).reshape(-1).astype(jnp.float32)
    up_full, down_full = gather_together((up_weight, down_weight), "fsdp", (1, 0))
    layer_out, grad_input, hidden, back_out = module_pass(
        features, keep, cotangent, gain_front, up_full, kernel_full, gain_back, down_full, span
    )
    local_rows = sent_and_summed(
        lax.dot_general(
            hidden, back_out, (((0,), (0,)), ((), ())), preferred_element_type=jnp.float32
        ).astype(jnp.bfloat16),
        "fsdp",
        0,
    )
    summed = lax.psum(local_rows, "dp")
    grad_down = summed / jnp.sqrt(jnp.float32(cotangent.shape[0] * groups * members))
    return (layer_out, grad_input, grad_down)


def solution(mesh):
    placed = (
        P(("dp", "fsdp"), None),
        P(("dp", "fsdp")),
        P(("dp", "fsdp")),
        P(None, "fsdp"),
        P(None, "fsdp"),
        P(None, "fsdp"),
        P(None, "fsdp"),
        P(None, "fsdp"),
        P(None, "fsdp"),
        P("fsdp"),
        P(None, "fsdp"),
        P(None, "fsdp"),
        P("fsdp"),
        P("fsdp", None),
        P(("dp", "fsdp"), None),
    )
    return jax.shard_map(
        local,
        mesh=mesh,
        in_specs=placed,
        out_specs=(P(("dp", "fsdp"), None), P(("dp", "fsdp"), None), P("fsdp", None)),
        check_vma=False,
    )
```

profile of v0, /device:TPU:0, one launch (start us, length us, event | category | flops | bytes accessed | tf_op | source)
XLA Modules:
  0.0 737.0 jit_solution(10071461535330743551)
XLA Ops:
  10.0 11.8 %all-to-all-start = ((s32[64,1,1]{2,1,0:T(1,128)}), s32[64,1,1]{2,1,0:T(1,128)}, u32[]{:S(2)}, u32[]{:S(2)}) async-start(s32[64,1,1]{2,1,0:T(1,128)} %copy.218), calls=%async_computation | async-start | bytes 65536 | tf_op jit(solution)/shard_map/all_to_all | solution.py:215
  24.1 10.4 %pad_maximum_fusion = bf16[1572864]{0:T(1024)(128)(2,1)} fusion(bf16[524288]{0:T(1024)(128)(2,1)S(1)} %bitcast.397, bf16[1048576]{0:T(1024)(128)(2,1)S(1)} %bitcast.392), kind=kLoop, calls=%fused_computation.103 | loop fusion | flops 6291456 | bytes 6291456 | tf_op jit(solution)/shard_map/concatenate | solution.py:29
  51.2 10.1 %all-to-all-start.1 = ((bf16[64,2,5120]{2,1,0:T(2,128)(2,1)}), bf16[64,2,5120]{2,1,0:T(2,128)(2,1)S(1)}, u32[]{:S(2)}, u32[]{:S(2)}) async-start(bf16[64,2,5120]{2,1,0:T(2,128)(2,1)} %reshape.638), calls=%async_computation.1 | async-start | bytes 2621440 | tf_op jit(solution)/shard_map/all_to_all | solution.py:214
  65.3 18.0 %all-to-all-done.1 = bf16[64,2,5120]{2,1,0:T(2,128)(2,1)S(1)} async-done(((bf16[64,2,5120]{2,1,0:T(2,128)(2,1)}), bf16[64,2,5120]{2,1,0:T(2,128)(2,1)S(1)}, u32[]{:S(2)}, u32[]{:S(2)}) %all-to-all-start.1) | async-done | bytes 1310752 | tf_op jit(solution)/shard_map/all_to_all | solution.py:214
  90.4 445.1 %while.10 = (s32[]{:T(128)}, bf16[2,256,2560]{2,1,0:T(8,128)(2,1)}, s32[2,16]{1,0:T(2,128)S(1)}, bf16[2,16,10240]{2,1,0:T(8,128)(2,1)}, bf16[9,256]{1,0:T(8,128)...) while((s32[]{:T(128)}, bf16[2,256,2560]{2,1,0:T(8,128)(2,1)}, ...), condition=%wide.region_4.5_spmd, body=%wide.region_3.4_spmd.sunk | while | flops 1972519936 | bytes 356025408 | solution.py:238
  146.4 54.4 %maximum_convert_fusion.2 = bf16[16,32,2,40,256]{4,1,3,0,2:T(8,128)(2,1)} fusion(f32[256]{0:T(256)S(1)} %bitcast.422, f32[16,32,2,40]{1,3,0,2:T(8,128)S(1)} %copy.284, f32[256]{0:T(256)S(1)} %bitcast.423, f32[16,32,2,40]{1,3,0,2:T(8,128)} %copy.286, f32[256]{0:T(256)S(1)} %bitcast.424, f32[16,32,2,40]{1,3,0,2:T(8,128)S(1)} %copy.289, ...), kind=kLoop, calls=%fused_computation.clone.1 | loop fusion | flops 199229440 | bytes 22455296 | tf_op jit(solution)/shard_map/while/body/eval_jaxpr/convert_element_type | solution.py:77
  200.8 17.6 %slice_bitcast_fusion.22 = (bf16[16,32,40,256]{3,1,2,0:T(8,128)(2,1)}, bf16[16,32,1,40,256]{4,1,3,0,2:T(8,128)(2,1)S(1)}, bf16[16,32,1,40,256]{4,1,3,0,2:T(8,128)(2,1)}) fusion(bf16[16,32,2,40,256]{4,1,3,0,2:T(8,128)(2,1)} %maximum_convert_fusion.2), kind=kLoop, calls=%fused_computation.89.clone.1 | loop fusion | bytes 52428800 | tf_op jit(solution)/shard_map/while/body/eval_jaxpr/squeeze | solution.py:53
  218.4 8.7 %concatenate.77 = bf16[16,32,40,256]{3,1,2,0:T(8,128)(2,1)S(1)} pad(bf16[16,31,40,256]{3,1,2,0:T(8,128)(2,1)} %bitcast.367, bf16[]{:T(256)} %constant.45.clone.7..sunk), padding=0_0x1_0x0_0x0_0 | pad | bytes 20643842 | tf_op jit(solution)/shard_map/while/body/eval_jaxpr/concatenate | solution.py:54
  235.5 5.6 slice_bitcast_fusion.23
  241.1 5.3 slice.620
  249.6 5.3 slice.621
  254.9 14.6 %fusion.121 = bf16[16,32,20,256]{3,1,2,0:T(8,128)(2,1)} fusion(bf16[16,32,20,2,256]{4,1,3,2,0:T(8,128)(2,1)} %bitcast.366, bf16[16,32,20,2,256]{4,1,3,2,0:T(8,128)(2,1)S(1)} %bitcast.364, bf16[16,32,20,2,256]{4,1,3,2,0:T(8,128)(2,1)S(1)} %bitcast.362, f32[256]{0:T(256)S(1)} %bitcast.410, f32[256]{0:T(256)S(1)} %bitcast.409, f32[256]{0:T(256)S(1)} %bitcast.408, ...), kind=kLoop, calls=%fused_computation.6.clone.1 | loop fusion | flops 70778880 | bytes 51651584 | tf_op jit(solution)/shard_map/while/body/eval_jaxpr/convert_element_type | solution.py:90
  269.5 8.9 %copy.307 = bf16[16,32,20,256]{3,2,1,0:T(8,128)(2,1)} copy(bf16[16,32,20,256]{3,1,2,0:T(8,128)(2,1)} %fusion.121) | data formatting | bytes 10485760 | tf_op jit(solution)/shard_map/while/body/eval_jaxpr/convert_element_type | solution.py:90
  278.4 9.0 %reshape.645 = bf16[10240,256]{1,0:T(8,128)(2,1)} reshape(bf16[16,32,20,256]{3,2,1,0:T(8,128)(2,1)} %copy.307) | data formatting | bytes 10485760 | tf_op jit(solution)/shard_map/while/body/eval_jaxpr/reshape | solution.py:95
  287.4 6.3 fusion.122
  293.6 8.9 %reshape.646 = bf16[16,16,2,20,256]{4,3,2,1,0:T(8,128)(2,1)} reshape(bf16[10240,256]{1,0:T(8,128)(2,1)} %fusion.122) | data formatting | bytes 10485760 | tf_op jit(solution)/shard_map/while/body/eval_jaxpr/reshape;while/body/eval_jaxpr/reshape | solution.py:51
  355.1 54.4 %maximum_convert_fusion.2 = bf16[16,32,2,40,256]{4,1,3,0,2:T(8,128)(2,1)} fusion(f32[256]{0:T(256)S(1)} %bitcast.422, f32[16,32,2,40]{1,3,0,2:T(8,128)S(1)} %copy.284, f32[256]{0:T(256)S(1)} %bitcast.423, f32[16,32,2,40]{1,3,0,2:T(8,128)} %copy.286, f32[256]{0:T(256)S(1)} %bitcast.424, f32[16,32,2,40]{1,3,0,2:T(8,128)S(1)} %copy.289, ...), kind=kLoop, calls=%fused_computation.clone.1 | loop fusion | flops 199229440 | bytes 22455296 | tf_op jit(solution)/shard_map/while/body/eval_jaxpr/convert_element_type | solution.py:77
  409.5 17.6 %slice_bitcast_fusion.22 = (bf16[16,32,40,256]{3,1,2,0:T(8,128)(2,1)}, bf16[16,32,1,40,256]{4,1,3,0,2:T(8,128)(2,1)S(1)}, bf16[16,32,1,40,256]{4,1,3,0,2:T(8,128)(2,1)}) fusion(bf16[16,32,2,40,256]{4,1,3,0,2:T(8,128)(2,1)} %maximum_convert_fusion.2), kind=kLoop, calls=%fused_computation.89.clone.1 | loop fusion | bytes 52428800 | tf_op jit(solution)/shard_map/while/body/eval_jaxpr/squeeze | solution.py:53
  427.1 8.7 %concatenate.77 = bf16[16,32,40,256]{3,1,2,0:T(8,128)(2,1)S(1)} pad(bf16[16,31,40,256]{3,1,2,0:T(8,128)(2,1)} %bitcast.367, bf16[]{:T(256)} %constant.45.clone.7..sunk), padding=0_0x1_0x0_0x0_0 | pad | bytes 20643842 | tf_op jit(solution)/shard_map/while/body/eval_jaxpr/concatenate | solution.py:54
  444.2 5.6 slice_bitcast_fusion.23
  458.2 5.3 slice.621
  463.5 14.6 %fusion.121 = bf16[16,32,20,256]{3,1,2,0:T(8,128)(2,1)} fusion(bf16[16,32,20,2,256]{4,1,3,2,0:T(8,128)(2,1)} %bitcast.366, bf16[16,32,20,2,256]{4,1,3,2,0:T(8,128)(2,1)S(1)} %bitcast.364, bf16[16,32,20,2,256]{4,1,3,2,0:T(8,128)(2,1)S(1)} %bitcast.362, f32[256]{0:T(256)S(1)} %bitcast.410, f32[256]{0:T(256)S(1)} %bitcast.409, f32[256]{0:T(256)S(1)} %bitcast.408, ...), kind=kLoop, calls=%fused_computation.6.clone.1 | loop fusion | flops 70778880 | bytes 51651584 | tf_op jit(solution)/shard_map/while/body/eval_jaxpr/convert_element_type | solution.py:90
  478.2 8.9 %copy.307 = bf16[16,32,20,256]{3,2,1,0:T(8,128)(2,1)} copy(bf16[16,32,20,256]{3,1,2,0:T(8,128)(2,1)} %fusion.121) | data formatting | bytes 10485760 | tf_op jit(solution)/shard_map/while/body/eval_jaxpr/convert_element_type | solution.py:90
  487.1 9.0 %reshape.645 = bf16[10240,256]{1,0:T(8,128)(2,1)} reshape(bf16[16,32,20,256]{3,2,1,0:T(8,128)(2,1)} %copy.307) | data formatting | bytes 10485760 | tf_op jit(solution)/shard_map/while/body/eval_jaxpr/reshape | solution.py:95
  496.0 6.3 fusion.122
  502.3 8.9 %reshape.646 = bf16[16,16,2,20,256]{4,3,2,1,0:T(8,128)(2,1)} reshape(bf16[10240,256]{1,0:T(8,128)(2,1)} %fusion.122) | data formatting | bytes 10485760 | tf_op jit(solution)/shard_map/while/body/eval_jaxpr/reshape;while/body/eval_jaxpr/reshape | solution.py:51
  535.6 6.2 convert_reduce_fusion.1
  542.3 6.9 reshape.629
  558.1 6.2 copy.221
  590.2 5.7 all_to_all.29
  598.9 5.5 multiply_reduce_fusion.2
  610.5 116.3 %all-reduce.16.cloned.1.call-done = f32[512,1024]{1,0:T(8,128)} async-done(((f32[512,1024]{1,0:T(8,128)}), f32[512,1024]{1,0:T(8,128)}) %all-reduce.16.cloned.1.call-update) | async-done | bytes 2097168 | tf_op jit(solution)/shard_map/psum | solution.py:263
  (305 shorter events, 213.0 us)
Async XLA Ops:
  7.2 32.2 %copy-start = (bf16[64,10240]{1,0:T(8,128)(2,1)S(1)}, bf16[64,10240]{1,0:T(8,128)(2,1)}, u32[]{:S(2)}) copy-start(bf16[64,10240]{1,0:T(8,128)(2,1)} %param.17) | copy-start | bytes 3932164
  7.2 15.4 %copy-start.10 = (bf16[1024,1024]{1,0:T(8,128)(2,1)S(1)}, bf16[1024,1024]{1,0:T(8,128)(2,1)}, u32[]{:S(2)}) copy-start(bf16[1024,1024]{1,0:T(8,128)(2,1)} %param.27) | copy-start | bytes 6291460
  10.0 41.2 %all-to-all-start = ((s32[64,1,1]{2,1,0:T(1,128)}), s32[64,1,1]{2,1,0:T(1,128)}, u32[]{:S(2)}, u32[]{:S(2)}) async-start(s32[64,1,1]{2,1,0:T(1,128)} %copy.218), calls=%async_computation | async-start | bytes 65536 | tf_op jit(solution)/shard_map/all_to_all | solution.py:215
  21.8 513.8 %all-gather.6.cloned.1.call-start = ((), (), s32[]{:S(2)}) async-start(), calls=%async_computation.3 | async-start | bytes 7864320 | tf_op jit(solution)/shard_map/all_gather | solution.py:248
  22.6 519.7 %all-gather.8.cloned.1.call-start = ((), (), s32[]{:S(2)}) async-start(), calls=%async_computation.5 | async-start | bytes 9437184 | tf_op jit(solution)/shard_map/all_gather | solution.py:30
  34.5 4.8 copy-start.38
  34.5 4.8 copy-start.40
  35.4 4.4 copy-start.41
  35.4 6.3 copy-start.33
  35.4 8.8 %copy-start.42 = (bf16[512]{0:T(512)(128)(2,1)S(1)}, bf16[512]{0:T(512)(128)(2,1)}, u32[]{:S(2)}) copy-start(bf16[512]{0:T(512)(128)(2,1)} %param.29) | copy-start | bytes 3076
  51.2 32.1 %all-to-all-start.1 = ((bf16[64,2,5120]{2,1,0:T(2,128)(2,1)}), bf16[64,2,5120]{2,1,0:T(2,128)(2,1)S(1)}, u32[]{:S(2)}, u32[]{:S(2)}) async-start(bf16[64,2,5120]{2,1,0:T(2,128)(2,1)} %reshape.638), calls=%async_computation.1 | async-start | bytes 2621440 | tf_op jit(solution)/shard_map/all_to_all | solution.py:214
  61.3 665.5 %all-reduce.16.cloned.1.call-start = ((), (), s32[]{:S(2)}) async-start(), calls=%async_computation.4 | async-start | bytes 4194304 | tf_op jit(solution)/shard_map/psum | solution.py:263
  64.8 25.7 %copy-start.29 = (f32[512]{0:T(512)}, f32[512]{0:T(512)S(1)}, u32[]{:S(2)}) copy-start(f32[512]{0:T(512)S(1)} %reshape.619) | copy-start | bytes 6148
  111.0 5.2 copy-start.43
  111.1 143.8 %copy-start.16 = (bf16[9,256]{1,0:T(8,128)(2,1)}, bf16[9,256]{1,0:T(8,128)(2,1)S(1)}, u32[]{:S(2)}) copy-start(bf16[9,256]{1,0:T(8,128)(2,1)S(1)} %get-tuple-element.321) | copy-start | bytes 13828 | tf_op jit(solution)/shard_map/while
  317.0 2.7 copy-start.17
  317.0 2.7 copy-start.44
  319.7 5.2 copy-start.43
  319.7 143.8 %copy-start.16 = (bf16[9,256]{1,0:T(8,128)(2,1)}, bf16[9,256]{1,0:T(8,128)(2,1)S(1)}, u32[]{:S(2)}) copy-start(bf16[9,256]{1,0:T(8,128)(2,1)S(1)} %get-tuple-element.321) | copy-start | bytes 13828 | tf_op jit(solution)/shard_map/while
  525.7 2.7 copy-start.17
  525.7 2.7 copy-start.44
  541.8 22.5 %copy-start.7 = (bf16[512,1024]{1,0:T(8,128)(2,1)}, bf16[512,1024]{1,0:T(8,128)(2,1)S(1)}, u32[]{:S(2)}) copy-start(bf16[512,1024]{1,0:T(8,128)(2,1)S(1)} %get-tuple-element.146) | copy-start | bytes 3145732
  549.3 2.8 copy-start.4
  552.0 2.8 slice-start.2
  558.1 6.2 copy-start.32
  564.3 4.6 copy-start.30
  569.0 2.0 copy-start.5
  569.0 2.0 copy-start.20
  569.0 2.0 copy-start.21
  584.5 2.3 copy-start.6
  598.9 5.5 copy-start.15
  608.2 121.8 %copy-start.1 = (bf16[64,10240]{1,0:T(8,128)(2,1)S(1)}, bf16[64,10240]{1,0:T(8,128)(2,1)}, u32[]{:S(2)}) copy-start(bf16[64,10240]{1,0:T(8,128)(2,1)} %param.17) | copy-start | bytes 3932164
  (29 other events, 41.7 us)
Sparse Core Ops, SparseCore 0:
  24.3 19.1 all-gather.5
  45.1 20.8 all-gather.7
  597.8 128.9 all-reduce.15
where the time goes:
time: 749 us; the launch traced here: 737 us
  local copies, waits for them, and re-layouts  292 us (39%)
  other arithmetic  190 us (25%)
  waiting for transfers between devices  135 us (18%)
  matrix products  41.8 us (6%)
  loops' own time  28.4 us (4%)
  starting transfers between devices  22 us (3%)
  between operations  14.7 us (2%)
  blocking collectives  13.3 us (2%)
    psum x1, waiting for transfers between devices, local(): summed = lax.psum(local_rows, 'dp')  116 us
    convert_element_type x2, other arithmetic, first_section(): return jnp.maximum(summed, 0.0).astype(jnp.bfloat16)  109 us
    mul x36, local copies, waits for them, and re-layouts, first_section(): window[:, :, :, None] * weights[3 * i + j].astype(jnp.float32)  46.2 us
    squeeze x4, local copies, waits for them, and re-layouts, phase_rows(): odd = split[:, :, 1]  42.2 us
    slice x16, local copies, waits for them, and re-layouts, phase_cols(): odd[:, :, :-1]  34.4 us
    convert_element_type x4, other arithmetic, depth_stride(): return summed.astype(jnp.bfloat16)  33.9 us
    another operation x1, loops' own time, local(): lax.map(sub_block, (panels.reshape(panel_count // per_block, per_block, -...  28.4 us
    squeeze x12, local copies, waits for them, and re-layouts, phase_cols(): odd = split[:, :, :, 1]  24.9 us
  transfers between devices with their start and end apart: 5, of which 2 were waited for; matrix products, arithmetic and copies ran while one was open for 62% of the time, Pallas kernels for 0%

commit v1 on v0

v1 whole, which is shorter than its diff:
```python
import functools
import math

import jax
import jax.numpy as jnp
from jax import lax
from jax.experimental import pallas as pl
from jax.experimental.pallas import tpu as pltpu
from jax.sharding import PartitionSpec as P

MELS = 80
PANEL = 128
EPSILON = 1e-05
SPAN = 16
GROUP = 8 * MELS
N_DP = 64
U_DEV = 32
ROWS = U_DEV * SPAN
D = 1024
CH = 256
HALF = CH // 2
MARK = 64.0
MESH = pl.DeviceIdType.MESH
VMEM_SPEC = pl.BlockSpec(memory_space=pltpu.VMEM)
ANY_SPEC = pl.BlockSpec(memory_space=pl.ANY)
BF = jnp.bfloat16
F32 = jnp.float32


def iota(shape, dim):
    return lax.broadcasted_iota(jnp.int32, shape, dim)


def dot(a, b):
    return jnp.dot(a, b, preferred_element_type=F32)


def shifted_peer(me, step):
    x = (me + step) % 4
    y = (me // 4 + step // 4) % 4
    z = (me // 16 + step // 16) % 4
    return z * 16 + y * 4 + x


N_SMALL = 8
N_BIG = 3


def exchange_kernel(*refs):
    frames, target, mel = refs[:3]
    small = refs[3 : 3 + N_SMALL]
    big = refs[11:14]
    windows, keep_out, band_out = refs[14:17]
    small_full = refs[17 : 17 + N_SMALL]
    big_other = refs[25:28]
    flat, outgoing, incoming = refs[28:31]
    small_other = refs[31 : 31 + N_SMALL]
    small_send, small_recv, big_send, big_recv, send_sem, recv_sem = refs[39:]

    me = lax.axis_index("dp")
    core = lax.axis_index("fsdp")
    other = 1 - core
    barrier = pltpu.get_barrier_semaphore()
    pl.semaphore_signal(barrier, inc=1, device_id=(me, other), device_id_type=MESH)

    def greet(step, carry):
        pl.semaphore_signal(
            barrier, inc=1, device_id=(shifted_peer(me, step), core), device_id_type=MESH
        )
        return carry

    lax.fori_loop(1, N_DP, greet, 0)

    picks = (target[...] == iota((N_DP, 64), 0)) & (frames[...] > 0)
    length = jnp.sum(jnp.where(picks, frames[...], 0), axis=1, keepdims=True)
    chosen = jnp.where(picks, 1.0, 0.0).astype(BF)
    for g in range(SPAN):
        rows = dot(chosen, mel[:, g * GROUP : (g + 1) * GROUP])
        rows = jnp.where(length > 8 * g, rows, MARK)
        for k in range(GROUP // 128):
            flat[k, pl.ds(g, N_DP, stride=SPAN), :] = rows[:, k * 128 : (k + 1) * 128]
    for k in range(GROUP // 128):
        outgoing[:, :, k * 128 : (k + 1) * 128] = flat[k].reshape(N_DP, SPAN, 128).astype(BF)

    pl.semaphore_wait(barrier, N_DP)

    partner = []
    for k in range(N_SMALL):
        copy = pltpu.make_async_remote_copy(
            src_ref=small[k],
            dst_ref=small_other[k],
            send_sem=small_send.at[k],
            recv_sem=small_recv.at[k],
            device_id=(me, other),
            device_id_type=MESH,
        )
        copy.start()
        partner.append(copy)

    def send(step, carry):
        pltpu.make_async_remote_copy(
            src_ref=outgoing.at[shifted_peer(me, step)],
            dst_ref=incoming.at[me],
            send_sem=send_sem,
            recv_sem=recv_sem,
            device_id=(shifted_peer(me, step), core),
            device_id_type=MESH,
        ).start()
        return carry

    lax.fori_loop(1, N_DP, send, 0)
    for k in range(N_BIG):
        copy = pltpu.make_async_remote_copy(
            src_ref=big[k],
            dst_ref=big_other[k],
            send_sem=big_send.at[k],
            recv_sem=big_recv.at[k],
            device_id=(me, other),
            device_id_type=MESH,
        )
        copy.start()
        partner.append(copy)
    incoming[pl.ds(me, 1)] = outgoing[pl.ds(me, 1)]

    for k in range(N_SMALL):
        partner[k].wait()
        width = small[k].shape[1]
        small_full[k][:, pl.ds(pl.multiple_of(core * width, 128), width)] = small[k][...]
        small_full[k][:, pl.ds(pl.multiple_of(other * width, 128), width)] = small_other[k][...]

    taps = small_full[0][...]
    row = iota((256, 9), 0)
    tap = iota((256, 9), 1)
    base = row - 80 * (tap // 3) - tap % 3 + 1

    def band(f, carry):
        b = base + (tap % 3) - 1
        hit = (base == 2 * f) & (b >= 0) & (b < MELS)
        column = dot(jnp.where(hit, 1.0, 0.0).astype(BF), taps)
        band_out[:, pl.ds(pl.multiple_of(f * CH, CH), CH)] = column.astype(BF)
        return carry

    lax.fori_loop(0, MELS // 2, band, 0)

    sent = outgoing.at[pl.ds(0, N_DP - 1)]
    got = incoming.at[pl.ds(0, N_DP - 1)]
    pltpu.make_async_copy(got, got, recv_sem).wait()

    total = N_DP * SPAN
    panels = incoming[...].reshape(total, GROUP)
    first_lane = jnp.where(iota((8, GROUP), 1) == 0, 1.0, 0.0).astype(BF)
    heads = lax.dot_general(
        first_lane, panels, (((1,), (1,)), ((), ())), preferred_element_type=F32
    )
    live_row = jnp.where(heads < MARK / 2, 1.0, 0.0).astype(BF)
    pick_heads = jnp.where(iota((total, 64), 0) == SPAN * iota((total, 64), 1), 1.0, 0.0)
    present = dot(live_row, pick_heads.astype(BF)).astype(BF)
    before = jnp.where(iota((64, 64), 0) < iota((64, 64), 1), 1.0, 0.0).astype(BF)
    place = dot(present, before).astype(BF)
    spread = jnp.where(iota((64, total), 1) // SPAN == iota((64, total), 0), 1.0, 0.0).astype(BF)
    present_row = dot(present, spread)[:1]
    place_row = dot(place, spread)[:1].astype(jnp.int32)
    goal = jnp.where(
        present_row > 0.5, (iota((1, total), 1) % SPAN) * U_DEV + place_row, -1
    )
    move = jnp.where(iota((ROWS, total), 0) == goal, 1.0, 0.0).astype(BF)
    x = dot(move, panels)
    keep = x[:, :1] < MARK / 2
    x = jnp.where(keep, x, 0.0)
    keep_out[...] = jnp.broadcast_to(jnp.where(keep, 1.0, 0.0), (ROWS, 128))

    late = jnp.concatenate([jnp.zeros((U_DEV, 128), F32), x[: ROWS - U_DEV, 512:]], axis=0)
    late = pltpu.roll(late, 80, 1)
    now = pltpu.roll(x[:, :256], 80, 1)
    lanes = iota((ROWS, 128), 1)
    w0 = jnp.concatenate([jnp.where(lanes < 80, late, now[:, :128]), now[:, 128:]], axis=1)
    windows[0:ROWS] = w0.astype(BF)
    windows[ROWS : 2 * ROWS] = pltpu.roll(x[:, :384], 384 - 80, 1)[:, :256].astype(BF)
    windows[2 * ROWS : 3 * ROWS] = pltpu.roll(x[:, 128:512], 384 - 112, 1)[:, :256].astype(BF)
    windows[3 * ROWS : 4 * ROWS] = pltpu.roll(x[:, 384:], 256 - 16, 1).astype(BF)

    pltpu.make_async_copy(sent, sent, send_sem).wait()
    for k in range(N_SMALL, N_SMALL + N_BIG):
        partner[k].wait()


def exchange(frames, target, mel, small, big):
    small_full = [jax.ShapeDtypeStruct((a.shape[0], 2 * a.shape[1]), BF) for a in small]
    shapes = [
        jax.ShapeDtypeStruct((4 * ROWS, 256), BF),
        jax.ShapeDtypeStruct((ROWS, 128), F32),
        jax.ShapeDtypeStruct((256, MELS // 2 * CH), BF),
        *small_full,
        *[jax.ShapeDtypeStruct(a.shape, BF) for a in big],
    ]
    out = pl.pallas_call(
        exchange_kernel,
        out_shape=shapes,
        in_specs=[VMEM_SPEC] * (3 + N_SMALL) + [ANY_SPEC] * N_BIG,
        out_specs=[VMEM_SPEC] * (3 + N_SMALL) + [ANY_SPEC] * N_BIG,
        scratch_shapes=[
            pltpu.VMEM((GROUP // 128, N_DP * SPAN, 128), F32),
            pltpu.VMEM((N_DP, SPAN, GROUP), BF),
            pltpu.VMEM((N_DP, SPAN, GROUP), BF),
            *[pltpu.VMEM(a.shape, BF) for a in small],
            pltpu.SemaphoreType.DMA((N_SMALL,)),
            pltpu.SemaphoreType.DMA((N_SMALL,)),
            pltpu.SemaphoreType.DMA((N_BIG,)),
            pltpu.SemaphoreType.DMA((N_BIG,)),
            pltpu.SemaphoreType.DMA,
            pltpu.SemaphoreType.DMA,
        ],
        compiler_params=pltpu.CompilerParams(
            collective_id=0, has_side_effects=True, vmem_limit_bytes=48 << 20
        ),
        name="exchange",
    )(frames, target, mel, *small, *big)
    return out[0], out[1], out[2], out[3 : 3 + N_SMALL], out[3 + N_SMALL :]


CHUNK = 64
PAD = U_DEV


def depth_rows(load, taps, r):
    total = None
    for i in range(3):
        for j in range(3):
            term = load(i, j, r) * taps[3 * i + j]
            total = term if total is None else total + term
    return total


def subsample_kernel(
    windows, band, depth_a, point_a, depth_b, point_b, linear_own, linear_other, out,
    first, spread_a, second, spread_b, fourth, linear, sems
):
    core = lax.axis_index("fsdp")
    width = D // 2
    loads = [
        pltpu.make_async_copy(
            linear_own, linear.at[:, pl.ds(pl.multiple_of(core * width, width), width)], sems.at[0]
        ),
        pltpu.make_async_copy(
            linear_other,
            linear.at[:, pl.ds(pl.multiple_of((1 - core) * width, width), width)],
            sems.at[1],
        ),
    ]
    for copy in loads:
        copy.start()
    first[:, 0] = jnp.zeros((4, PAD + ROWS, CH), BF)
    second[:, 0] = jnp.zeros((2, PAD + ROWS, CH), BF)
    for col in range(1, 5):
        first[3, col, 0:PAD] = jnp.zeros((PAD, CH), BF)
    for col in range(1, 3):
        second[1, col, 0:PAD] = jnp.zeros((PAD, CH), BF)
    taps_a = [jnp.broadcast_to(depth_a[k : k + 1], (CHUNK, CH)) for k in range(9)]
    taps_b = [jnp.broadcast_to(depth_b[k : k + 1], (CHUNK, CH)) for k in range(9)]

    def step(n, carry):
        for t in range(4):
            x = windows[t * ROWS : (t + 1) * ROWS]
            for f in range(4):
                w = band[:, pl.ds(pl.multiple_of(n * 4 * CH + f * CH, CH), CH)]
                first[t, 1 + f, PAD : PAD + ROWS] = jnp.maximum(dot(x, w), 0.0).astype(BF)
        for t2 in range(2):
            for f2 in range(2):

                def load(i, j, r):
                    t = 2 * t2 + i - 1
                    if t < 0:
                        return first[3, 2 * f2 + j, r : r + CHUNK]
                    return first[t, 2 * f2 + j, PAD + r : PAD + r + CHUNK]

                for r in range(0, ROWS, CHUNK):
                    spread_a[r : r + CHUNK] = depth_rows(load, taps_a, r)
                mapped = dot(spread_a[...], point_a[...])
                second[t2, 1 + f2, PAD : PAD + ROWS] = jnp.maximum(mapped, 0.0).astype(BF)

        def load_b(i, j, r):
            if i == 0:
                return second[1, j, r : r + CHUNK]
            return second[i - 1, j, PAD + r : PAD + r + CHUNK]

        for r in range(0, ROWS, CHUNK):
            spread_b[r : r + CHUNK] = depth_rows(load_b, taps_b, r)
        mapped = dot(spread_b[...], point_b[...])
        fourth[:, pl.ds(pl.multiple_of(n * CH, CH), CH)] = jnp.maximum(mapped, 0.0).astype(BF)
        for t in range(4):
            first[t, 0] = first[t, 4]
        for t2 in range(2):
            second[t2, 0] = second[t2, 2]
        return carry

    lax.fori_loop(0, 10, step, 0)
    for copy in loads:
        copy.wait()
    out[...] = dot(fourth[...], linear[...]).astype(BF)


def subsample(windows, band, depth_a, point_a, depth_b, point_b, linear_own, linear_other):
    return pl.pallas_call(
        subsample_kernel,
        out_shape=jax.ShapeDtypeStruct((ROWS, D), BF),
        in_specs=[VMEM_SPEC] * 6 + [ANY_SPEC] * 2,
        out_specs=VMEM_SPEC,
        scratch_shapes=[
            pltpu.VMEM((4, 5, PAD + ROWS, CH), BF),
            pltpu.VMEM((ROWS, CH), BF),
            pltpu.VMEM((2, 3, PAD + ROWS, CH), BF),
            pltpu.VMEM((ROWS, CH), BF),
            pltpu.VMEM((ROWS, 10 * CH), BF),
            pltpu.VMEM((10 * CH, D), BF),
            pltpu.SemaphoreType.DMA((2,)),
        ],
        compiler_params=pltpu.CompilerParams(vmem_limit_bytes=56 << 20),
        name="subsample",
    )(windows, band, depth_a, point_a, depth_b, point_b, linear_own, linear_other)


def in_blocks(value, dim, size):
    before, after = (value.shape[:dim], value.shape[dim + 1 :])
    return jnp.moveaxis(value.reshape(*before, size, -1, *after), dim, 0)


def sent_and_summed(value, axis, dim):
    size = lax.axis_size(axis)
    tiles = lax.all_to_all(in_blocks(value, dim, size), axis, 0, 0, tiled=True)
    return jnp.sum(tiles.astype(jnp.float32), axis=0)


def depth_forward(gated, kernel, span):
    groups_in = gated.shape[0] // span
    half_width = kernel.shape[0] // 2
    shaped = jnp.pad(gated.reshape(groups_in, span, -1), ((0, 0), (half_width, half_width), (0, 0)))
    summed = jnp.zeros((groups_in, span, gated.shape[1]), jnp.float32)
    for k in range(kernel.shape[0]):
        summed = summed + shaped[:, k : k + span].astype(jnp.float32) * kernel[k].astype(
            jnp.float32
        )
    return summed.reshape(gated.shape[0], -1)


def depth_backward(upstream, kernel, span):
    groups_in = upstream.shape[0] // span
    half_width = kernel.shape[0] // 2
    shaped = jnp.pad(
        upstream.reshape(groups_in, span, -1), ((0, 0), (half_width, half_width), (0, 0))
    )
    summed = jnp.zeros((groups_in, span, upstream.shape[1]), jnp.float32)
    for k in range(kernel.shape[0]):
        offset = 2 * half_width - k
        summed = summed + shaped[:, offset : offset + span] * kernel[k].astype(jnp.float32)
    return summed.reshape(upstream.shape[0], -1)


def module_pass(
    features, keep, cotangent, norm_gain, up_weight, depth_kernel, conv_gain, down_weight, span
):
    width = features.shape[1]
    values = features.astype(jnp.float32)
    centred = values - jnp.mean(values, axis=1, keepdims=True)
    scale_one = lax.rsqrt(jnp.mean(centred * centred, axis=1, keepdims=True) + EPSILON)
    standard = centred * scale_one
    normed = (standard * norm_gain.astype(jnp.float32)).astype(jnp.bfloat16)
    projected = jnp.dot(normed, up_weight, preferred_element_type=jnp.float32)
    value_half = projected[:, :width]
    gate_half = jax.nn.sigmoid(projected[:, width:])
    row_keep = keep[:, None]
    gated = (row_keep * value_half * gate_half).astype(jnp.bfloat16)
    depthwise = depth_forward(gated, depth_kernel, span)
    centred_two = depthwise - jnp.mean(depthwise, axis=1, keepdims=True)
    scale_two = lax.rsqrt(jnp.mean(centred_two * centred_two, axis=1, keepdims=True) + EPSILON)
    standard_two = centred_two * scale_two
    active = standard_two * conv_gain.astype(jnp.float32)
    swish_gate = jax.nn.sigmoid(active)
    hidden = (active * swish_gate).astype(jnp.bfloat16)
    mixed = jnp.dot(hidden, down_weight, preferred_element_type=jnp.float32)
    layer_out = (row_keep * (values + mixed)).astype(jnp.bfloat16)
    back_out = jnp.where(row_keep > 0, cotangent, jnp.zeros_like(cotangent))
    back_hidden = lax.dot_general(
        back_out, down_weight, (((1,), (1,)), ((), ())), preferred_element_type=jnp.float32
    )
    back_active = back_hidden * (swish_gate + active * swish_gate * (1.0 - swish_gate))
    gain_back = back_active * conv_gain.astype(jnp.float32)
    back_depth = scale_two * (
        gain_back
        - jnp.mean(gain_back, axis=1, keepdims=True)
        - standard_two * jnp.mean(gain_back * standard_two, axis=1, keepdims=True)
    )
    back_gated = row_keep * depth_backward(back_depth, depth_kernel, span)
    back_proj = jnp.concatenate(
        [back_gated * gate_half, back_gated * value_half * gate_half * (1.0 - gate_half)], axis=1
    ).astype(jnp.bfloat16)
    back_normed = lax.dot_general(
        back_proj, up_weight, (((1,), (1,)), ((), ())), preferred_element_type=jnp.float32
    )
    gain_front = back_normed * norm_gain.astype(jnp.float32)
    back_input = scale_one * (
        gain_front
        - jnp.mean(gain_front, axis=1, keepdims=True)
        - standard * jnp.mean(gain_front * standard, axis=1, keepdims=True)
    )
    grad_input = (back_out.astype(jnp.float32) + back_input).astype(jnp.bfloat16)
    return (layer_out, grad_input, hidden, back_out)


def by_panel(rows):
    return rows.reshape(SPAN, U_DEV, -1).transpose(1, 0, 2).reshape(ROWS, -1)


def joined(own, other, dim):
    order = lax.axis_index("fsdp") == 0
    first = jnp.where(order, own, other)
    last = jnp.where(order, other, own)
    return jnp.concatenate([first, last], axis=dim)


def local(
    mel_panels,
    frames,
    target,
    conv_first,
    depth_a,
    point_a,
    depth_b,
    point_b,
    linear_weight,
    norm_gain,
    up_weight,
    depth_kernel,
    conv_gain,
    down_weight,
    cotangent,
):
    small = (
        conv_first,
        depth_a,
        point_a,
        depth_b,
        point_b,
        norm_gain[None],
        depth_kernel,
        conv_gain[None],
    )
    big = (linear_weight, up_weight, down_weight)
    windows, keep, band, full, other = exchange(frames[None], target[None], mel_panels, small, big)
    features = subsample(windows, band, *full[1:5], linear_weight, other[0])
    features = by_panel(features)
    keep = by_panel(keep)[:, 0]
    layer_out, grad_input, hidden, back_out = module_pass(
        features,
        keep,
        cotangent,
        full[5][0],
        joined(up_weight, other[1], 1),
        full[6],
        full[7][0],
        joined(down_weight, other[2], 0),
        SPAN,
    )
    local_rows = sent_and_summed(
        lax.dot_general(
            hidden, back_out, (((0,), (0,)), ((), ())), preferred_element_type=jnp.float32
        ).astype(jnp.bfloat16),
        "fsdp",
        0,
    )
    summed = lax.psum(local_rows, "dp")
    grad_down = summed / jnp.sqrt(jnp.float32(ROWS * N_DP * 2))
    return (layer_out, grad_input, grad_down)


def solution(mesh):
    placed = (
        P(("dp", "fsdp"), None),
        P(("dp", "fsdp")),
        P(("dp", "fsdp")),
        P(None, "fsdp"),
        P(None, "fsdp"),
        P(None, "fsdp"),
        P(None, "fsdp"),
        P(None, "fsdp"),
        P(None, "fsdp"),
        P("fsdp"),
        P(None, "fsdp"),
        P(None, "fsdp"),
        P("fsdp"),
        P("fsdp", None),
        P(("dp", "fsdp"), None),
    )
    return jax.shard_map(
        local,
        mesh=mesh,
        in_specs=placed,
        out_specs=(P(("dp", "fsdp"), None), P(("dp", "fsdp"), None), P("fsdp", None)),
        check_vma=False,
    )
```

time: 749 us -> 254 us (0.34); the launches traced: 737 us -> 254 us
  local copies, waits for them, and re-layouts: 292 us -> 22.3 us
  other arithmetic: 190 us -> 23.2 us
  Pallas kernels: 0 us -> 65.1 us
  matrix products: 41.8 us -> 10.7 us
  loops' own time: 28.4 us -> 0 us
  waiting for transfers between devices: 135 us -> 113 us
  starting transfers between devices: 22 us -> 0.04 us
  blocking collectives: 13.3 us -> 5.42 us
    convert_element_type x14 -> x1, other arithmetic: 145 us -> 1.57 us  [module_pass(): values = features.astype(jnp.float32)]
    squeeze x16 -> x0, local copies, waits for them, and re-layouts: 67.1 us -> none  [the longest x4 42.2 us: phase_rows(): odd = split[:, :, 1]]
    pallas_call x0 -> x2, Pallas kernels: none -> 65.1 us  [the longest x1 35.2 us: exchange(): pl.pallas_call(exchange_kernel, out_shape=shapes, in_specs=[VMEM_SPEC] *...]
    slice x37 -> x1, local copies, waits for them, and re-layouts: 49.4 us -> 0.14 us  [local(): keep = by_panel(keep)[:, 0]]
    mul x36 -> x0, local copies, waits for them, and re-layouts: 46.2 us -> none  [first_section(): window[:, :, :, None] * weights[3 * i + j].astype(jnp.float32)]
    reshape x9 -> x1, local copies, waits for them, and re-layouts: 38.1 us -> 0.16 us  [by_panel(): return rows.reshape(SPAN, U_DEV, -1).transpose(1, 0, 2).reshape(ROWS, -1)]
    another operation x1 -> x0, loops' own time: 28.4 us -> none  [local(): lax.map(sub_block, (panels.reshape(panel_count // per_block, per_block, -...]
    dot_general x7 -> x0, matrix products: 25.6 us -> none  [the longest x4 15.4 us: point_relu(): jnp.dot(spread.reshape(-1, shape_in[3]), weights, preferred_element_type=...]
  transfers between devices with their start and end apart: 5 -> 1, of which waited for: 2 -> 1; matrix products, arithmetic and copies ran while one was open for 62% -> 5% of each run, Pallas kernels for 0% -> 0%
where the time goes in v1:
time: 254 us
  waiting for transfers between devices  113 us (44%)
  Pallas kernels  65.1 us (26%)
  other arithmetic  23.2 us (9%)
  local copies, waits for them, and re-layouts  22.3 us (9%)
  between operations  14.4 us (6%)
  matrix products  10.7 us (4%)
  blocking collectives  5.42 us (2%)
    psum x1, waiting for transfers between devices, local(): summed = lax.psum(local_rows, 'dp')  113 us
    pallas_call x1, Pallas kernels, exchange(): pl.pallas_call(exchange_kernel, out_shape=shapes, in_specs=[VMEM_SPEC] *...  35.2 us
    pallas_call x1, Pallas kernels, subsample(): pl.pallas_call(subsample_kernel, out_shape=jax.ShapeDtypeStruct((ROWS, D)...  29.8 us
    unnamed x62, local copies, waits for them, and re-layouts  17.1 us
    all_to_all x1, blocking collectives, sent_and_summed(): tiles = lax.all_to_all(in_blocks(value, dim, size), axis, 0, 0, tiled=True)  5.42 us
  transfers between devices with their start and end apart: 1, of which 1 were waited for; matrix products, arithmetic and copies ran while one was open for 5% of the time, Pallas kernels for 0%

profile of v1, /device:TPU:0, one launch (start us, length us, event | category | flops | bytes accessed | tf_op | source)
XLA Modules:
  0.0 253.8 jit_solution(9387528093217872680)
XLA Ops:
  8.6 1.2 copy-done
  9.8 1.3 copy-done.2
  11.1 0.8 copy-done.6
  12.0 0.8 copy-done.7
  12.8 0.7 copy-done.8
  13.5 0.7 copy-done.11
  16.9 35.2 %exchange.1 = (bf16[2048,256]{1,0:T(8,128)(2,1)S(1)}, f32[512,128]{1,0:T(8,128)S(1)}, bf16[256,10240]{1,0:T(8,128)(2,1)}, bf16[9,256]{1,0:T(8,128)(2,1)}, bf16[9...) custom-call(s32[1,64]{1,0:T(1,128)S(1)} %bitcast.58, ...), custom_call_target="tpu_custom_call" | custom-call | tf_op jit(solution)/shard_map/exchange/pallas_call | solution.py:196
  52.1 1.0 copy-done.3
  54.1 29.8 %subsample.1 = bf16[512,1024]{1,0:T(8,128)(2,1)} custom-call(bf16[2048,256]{1,0:T(8,128)(2,1)} %copy-done.3, bf16[256,10240]{1,0:T(8,128)(2,1)} %get-tuple-element.18.band, bf16[9,256]{1,0:T(8,128)(2,1)} %copy-done.9, bf16[256,256]{1,0:T(8,128)(2,1)} %copy-done.4, bf16[9,256]{1,0:T(8,128)(2,1)} %copy-done.10, bf16[256,256]{1,0:T(8,128)(2,1)} %copy-done.5, ...), custom_call_target="tpu_custom_call" | custom-call | tf_op jit(solution)/shard_map/subsample/pallas_call | solution.py:303
  83.9 1.5 fusion.29
  85.5 1.6 multiply_reduce_fusion.3
  87.2 1.6 convert_bitcast_fusion
  89.1 2.8 %copy.31 = f32[32,16,1024]{2,1,0:T(8,128)S(1)} copy(f32[32,16,1024]{2,0,1:T(8,128)} %convert_bitcast_fusion) | data formatting | bytes 4194304 | tf_op jit(solution)/shard_map/convert_element_type | solution.py:362
  91.9 3.3 %broadcast_select_fusion.1 = (bf16[1024,1024]{1,0:T(8,128)(2,1)S(1)}, bf16[1024,1024]{1,0:T(8,128)(2,1)S(1)}) fusion(bf16[1024,1024]{1,0:T(8,128)(2,1)} %refs_12_.1, bf16[1024,1024]{1,0:T(8,128)(2,1)} %get-tuple-element.25, pred[]{:T(512)S(6)} %eq.4), kind=kLoop, calls=%fused_computation.67 | loop fusion | flops 2097152 | bytes 8388609 | tf_op jit(solution)/shard_map/jit(_where)/select_n | solution.py:415
  95.5 2.4 fusion.1
  98.5 1.3 copy-done.20
  99.9 2.7 %fusion.37 = (f32[32,16]{1,0:T(8,128)S(1)}, f32[32,16,1024]{2,1,0:T(8,128)S(1)}) fusion(f32[1024]{0:T(1024)S(1)} %bitcast.69, f32[1024]{0:T(1024)S(1)} %bitcast.71, f32[1024]{0:T(1024)S(1)} %bitcast.73, f32[1024]{0:T(1024)S(1)} %bitcast.75, f32[1024]{0:T(1024)S(1)} %bitcast.77, bf16[32,16,1024]{2,1,0:T(8,128)(2,1)S(1)} %bitcast.63, f32[1024]{0:T(1024)S(1)} %bitcast.79, ...), kind=kLoop, calls=%fused_computation.101 | loop fusion | flops 14155264 | bytes 3184640 | tf_op jit(solution)/shard_map/reduce_sum | solution.py:373
  103.9 0.7 copy-done.29
  104.7 1.4 convolution_convert_fusion
  106.1 5.4 %all_to_all.5 = bf16[2,512,1024]{2,1,0:T(8,128)(2,1)S(1)} all-to-all(bf16[2,512,1024]{2,1,0:T(8,128)(2,1)S(1)} %bitcast.66), channel_id=1, replica_groups=mesh['dp'=64,'fsdp'=2] {'fsdp'}, dimensions={0} | all-to-all | bytes 4194304 | tf_op jit(solution)/shard_map/all_to_all | solution.py:329
  111.5 1.8 convert_reduce_fusion
  113.3 1.2 copy-done.1
  114.7 1.4 copy-done.24
  116.4 2.0 fusion.36
  119.0 2.3 fusion.10
  121.3 0.8 multiply_convert_fusion.1
  122.1 0.8 copy-done.19
  124.1 2.6 %multiply_reduce_fusion.4 = (f32[512]{0:T(512)S(1)}, f32[512]{0:T(512)S(1)}, f32[512,1024]{1,0:T(8,128)S(1)}) fusion(f32[1024]{0:T(1024)S(1)} %bitcast.86, f32[512]{0:T(512)S(1)} %rsqrt.23, f32[512]{0:T(512)S(1)} %div.41, f32[32,16,1024]{2,1,0:T(8,128)S(1)} %copy-done.19, bf16[1024,1024]{1,0:T(8,128)(2,1)S(1)} %copy-done.28, ...), kind=kOutput, calls=%fused_computation.71 | convolution fusion | flops 2163211264 | bytes 10498048 | tf_op jit(solution)/shard_map/dot_general | solution.py:396
  126.8 2.0 add_convert_fusion
  128.8 2.3 fusion.27
  131.0 112.7 %all-reduce.4.cloned.1.call-done = f32[512,1024]{1,0:T(8,128)} async-done(((f32[512,1024]{1,0:T(8,128)}), f32[512,1024]{1,0:T(8,128)}) %all-reduce.4.cloned.1.call-update) | async-done | bytes 2097168 | tf_op jit(solution)/shard_map/psum | solution.py:470
  243.7 3.2 %broadcast_multiply_fusion = f32[512,1024]{1,0:T(8,128)} fusion(f32[512,1024]{1,0:T(8,128)} %all-reduce.4.cloned.1.call-done), kind=kLoop, calls=%fused_computation.73 | loop fusion | flops 524288 | bytes 4194304 | tf_op jit(solution)/shard_map/div | solution.py:471
  (83 shorter events, 9.9 us)
Async XLA Ops:
  7.2 236.5 %all-reduce.4.cloned.1.call-start = ((), (), s32[]{:S(2)}) async-start(), calls=%async_computation.1 | async-start | bytes 4194304 | tf_op jit(solution)/shard_map/psum | solution.py:470
  8.6 1.2 copy-start
  9.8 1.3 copy-start.2
  11.1 0.8 copy-start.6
  12.0 0.8 copy-start.7
  12.8 0.7 copy-start.8
  13.5 0.7 copy-start.11
  14.2 0.7 copy-start.12
  14.9 0.7 copy-start.13
  15.6 0.7 copy-start.14
  16.2 0.7 copy-start.15
  52.1 1.0 copy-start.3
  53.1 0.7 copy-start.4
  53.1 0.7 copy-start.5
  53.1 0.8 copy-start.9
  53.1 1.0 copy-start.10
  83.9 3.3 %copy-start.22 = (bf16[512,1024]{1,0:T(8,128)(2,1)S(1)}, bf16[512,1024]{1,0:T(8,128)(2,1)}, u32[]{:S(2)}) copy-start(bf16[512,1024]{1,0:T(8,128)(2,1)} %subsample.1) | copy-start | bytes 3145732
  91.9 3.3 %copy-start.18 = (f32[32,16,1024]{2,1,0:T(8,128)}, f32[32,16,1024]{2,1,0:T(8,128)S(1)}, u32[]{:S(2)}) copy-start(f32[32,16,1024]{2,1,0:T(8,128)S(1)} %copy.31) | copy-start | bytes 6291460
  95.2 2.7 %copy-start.25 = (bf16[1024,1024]{1,0:T(8,128)(2,1)}, bf16[1024,1024]{1,0:T(8,128)(2,1)S(1)}, u32[]{:S(2)}) copy-start(bf16[1024,1024]{1,0:T(8,128)(2,1)S(1)} %get-tuple-element.37) | copy-start | bytes 6291460
  95.2 2.7 %copy-start.27 = (bf16[1024,1024]{1,0:T(8,128)(2,1)}, bf16[1024,1024]{1,0:T(8,128)(2,1)S(1)}, u32[]{:S(2)}) copy-start(bf16[1024,1024]{1,0:T(8,128)(2,1)S(1)} %get-tuple-element.38) | copy-start | bytes 6291460
  97.9 1.9 copy-start.20
  102.6 1.3 copy-start.16
  103.4 1.2 copy-start.29
  103.9 2.2 copy-start.23
  113.3 1.2 copy-start.1
  114.5 1.6 copy-start.24
  114.5 1.9 copy-start.30
  116.4 2.0 copy-start.17
  118.9 2.3 copy-start.21
  121.3 1.6 copy-start.19
  121.3 2.2 copy-start.26
  121.3 2.8 %copy-start.28 = (bf16[1024,1024]{1,0:T(8,128)(2,1)S(1)}, bf16[1024,1024]{1,0:T(8,128)(2,1)}, u32[]{:S(2)}) copy-start(bf16[1024,1024]{1,0:T(8,128)(2,1)} %copy-done.27) | copy-start | bytes 6291460
Sparse Core Ops, SparseCore 0:
  113.5 130.1 all-reduce.3

commit v2 on v1

--- a/solution.py
+++ b/solution.py
@@ -319,102 +319,323 @@
     )(windows, band, depth_a, point_a, depth_b, point_b, linear_own, linear_other)
 
 
-def in_blocks(value, dim, size):
-    before, after = (value.shape[:dim], value.shape[dim + 1 :])
-    return jnp.moveaxis(value.reshape(*before, size, -1, *after), dim, 0)
-
-
-def sent_and_summed(value, axis, dim):
-    size = lax.axis_size(axis)
-    tiles = lax.all_to_all(in_blocks(value, dim, size), axis, 0, 0, tiled=True)
-    return jnp.sum(tiles.astype(jnp.float32), axis=0)
-
-
-def depth_forward(gated, kernel, span):
-    groups_in = gated.shape[0] // span
-    half_width = kernel.shape[0] // 2
-    shaped = jnp.pad(gated.reshape(groups_in, span, -1), ((0, 0), (half_width, half_width), (0, 0)))
-    summed = jnp.zeros((groups_in, span, gated.shape[1]), jnp.float32)
-    for k in range(kernel.shape[0]):
-        summed = summed + shaped[:, k : k + span].astype(jnp.float32) * kernel[k].astype(
-            jnp.float32
+def dot_t(a, b):
+    return lax.dot_general(a, b, (((1,), (1,)), ((), ())), preferred_element_type=F32)
+
+
+def dot_rows(a, b):
+    return lax.dot_general(a, b, (((0,), (0,)), ((), ())), preferred_element_type=F32)
+
+
+def row_mean(x):
+    return jnp.sum(x, axis=1, keepdims=True) * (1.0 / D)
+
+
+KER = 9
+BORDER = KER // 2 * U_DEV
+HALF_D = D // 2
+N_TILE = 256
+
+
+def lane_tile(n, start=0):
+    return pl.ds(pl.multiple_of(start + n * N_TILE, N_TILE), N_TILE)
+
+
+def module_kernel(
+    features, keep, cotangent, norm_gain, depth_kernel, conv_gain,
+    up_own, up_other, down_own, down_other,
+    layer_out, grad_input, grad_down,
+    up, down, normed, stats, gate_a, gate_b, gated, standard_two, slope, hidden, back_out,
+    grad_own, to_partner, from_partner, part, parts, mine, shared, big, back_depth, back_proj,
+    load_sems, partner_send, partner_recv, send_sems, recv_sems,
+):
+    me = lax.axis_index("dp")
+    core = lax.axis_index("fsdp")
+    other = 1 - core
+    barrier = pltpu.get_barrier_semaphore()
+    pl.semaphore_signal(barrier, inc=1, device_id=(me, other), device_id_type=MESH)
+
+    def greet(step, carry):
+        pl.semaphore_signal(
+            barrier, inc=1, device_id=(shifted_peer(me, step), core), device_id_type=MESH
         )
-    return summed.reshape(gated.shape[0], -1)
-
-
-def depth_backward(upstream, kernel, span):
-    groups_in = upstream.shape[0] // span
-    half_width = kernel.shape[0] // 2
-    shaped = jnp.pad(
-        upstream.reshape(groups_in, span, -1), ((0, 0), (half_width, half_width), (0, 0))
+        return carry
+
+    lax.fori_loop(1, N_DP, greet, 0)
+
+    def part_of(which, width):
+        return pl.ds(pl.multiple_of(which * width, width), width)
+
+    loads = [
+        pltpu.make_async_copy(up_own, up.at[:, part_of(core, D)], load_sems.at[0]),
+        pltpu.make_async_copy(up_other, up.at[:, part_of(other, D)], load_sems.at[1]),
+        pltpu.make_async_copy(down_own, down.at[part_of(core, HALF_D)], load_sems.at[2]),
+        pltpu.make_async_copy(down_other, down.at[part_of(other, HALF_D)], load_sems.at[3]),
+    ]
+    for copy in loads:
+        copy.start()
+
+    def rows_of(g, shift=0):
+        return pl.ds(pl.multiple_of((g + shift) * U_DEV, U_DEV), U_DEV)
+
+    gain_one = norm_gain[...].astype(F32)
+    gain_two = conv_gain[...].astype(F32)
+
+    def norm_rows(g, carry):
+        values = features[rows_of(g)].astype(F32)
+        mean = row_mean(values)
+        centred = values - mean
+        scale = lax.rsqrt(row_mean(centred * centred) + EPSILON)
+        normed[rows_of(g)] = (centred * scale * gain_one).astype(BF)
+        stats[0, rows_of(g)] = jnp.broadcast_to(mean, (U_DEV, 128))
+        stats[1, rows_of(g)] = jnp.broadcast_to(scale, (U_DEV, 128))
+        return carry
+
+    lax.fori_loop(0, SPAN, norm_rows, 0)
+    gated[0:BORDER] = jnp.zeros((BORDER, D), BF)
+    gated[BORDER + ROWS :] = jnp.zeros((BORDER, D), BF)
+    back_depth[0:BORDER] = jnp.zeros((BORDER, D), F32)
+    back_depth[BORDER + ROWS :] = jnp.zeros((BORDER, D), F32)
+
+    out_row = iota((ROWS, ROWS), 0)
+    in_row = iota((ROWS, ROWS), 1)
+    to_groups = jnp.where(in_row == (out_row % U_DEV) * SPAN + out_row // U_DEV, 1.0, 0.0)
+    to_groups = to_groups.astype(BF)
+    to_panels = jnp.where(in_row == (out_row % SPAN) * U_DEV + out_row // SPAN, 1.0, 0.0)
+    to_panels = to_panels.astype(BF)
+
+    loads[0].wait()
+    loads[1].wait()
+
+    def project(n, carry):
+        value = dot(normed[...], up[:, lane_tile(n)])
+        gate = jax.nn.sigmoid(dot(normed[...], up[:, lane_tile(n, D)]))
+        both = value * gate
+        gate_a[:, lane_tile(n)] = gate
+        gate_b[:, lane_tile(n)] = both * (1.0 - gate)
+        gated[BORDER : BORDER + ROWS, lane_tile(n)] = (keep[:, :1] * both).astype(BF)
+        moved = dot(to_groups, cotangent[:, lane_tile(n)])
+        back_out[:, lane_tile(n)] = jnp.where(keep[:, :1] > 0, moved, 0.0).astype(BF)
+        return carry
+
+    lax.fori_loop(0, D // N_TILE, project, 0)
+
+    def conv_rows(g, carry):
+        summed = None
+        for k in range(KER):
+            tap = depth_kernel[k : k + 1].astype(F32)
+            term = gated[rows_of(g, k)].astype(F32) * tap
+            summed = term if summed is None else summed + term
+        centred = summed - row_mean(summed)
+        scale = lax.rsqrt(row_mean(centred * centred) + EPSILON)
+        standard = centred * scale
+        active = standard * gain_two
+        swish = jax.nn.sigmoid(active)
+        act = active * swish
+        hidden[rows_of(g)] = act.astype(BF)
+        standard_two[rows_of(g)] = standard
+        slope[rows_of(g)] = (swish + act * (1.0 - swish)) * gain_two
+        stats[2, rows_of(g)] = jnp.broadcast_to(scale, (U_DEV, 128))
+        return carry
+
+    lax.fori_loop(0, SPAN, conv_rows, 0)
+
+    def grad_rows(which, n):
+        mine_rows = hidden[:, part_of(which, HALF_D)]
+        return dot_rows(mine_rows, back_out[:, lane_tile(n)])
+
+    def partner_grad(n, carry):
+        to_partner[:, lane_tile(n)] = grad_rows(other, n).astype(BF)
+        return carry
+
+    lax.fori_loop(0, D // N_TILE, partner_grad, 0)
+    pl.semaphore_wait(barrier, N_DP)
+    swap = pltpu.make_async_remote_copy(
+        src_ref=to_partner,
+        dst_ref=from_partner,
+        send_sem=partner_send,
+        recv_sem=partner_recv,
+        device_id=(me, other),
+        device_id_type=MESH,
     )
-    summed = jnp.zeros((groups_in, span, upstream.shape[1]), jnp.float32)
-    for k in range(kernel.shape[0]):
-        offset = 2 * half_width - k
-        summed = summed + shaped[:, offset : offset + span] * kernel[k].astype(jnp.float32)
-    return summed.reshape(upstream.shape[0], -1)
-
-
-def module_pass(
-    features, keep, cotangent, norm_gain, up_weight, depth_kernel, conv_gain, down_weight, span
-):
-    width = features.shape[1]
-    values = features.astype(jnp.float32)
-    centred = values - jnp.mean(values, axis=1, keepdims=True)
-    scale_one = lax.rsqrt(jnp.mean(centred * centred, axis=1, keepdims=True) + EPSILON)
-    standard = centred * scale_one
-    normed = (standard * norm_gain.astype(jnp.float32)).astype(jnp.bfloat16)
-    projected = jnp.dot(normed, up_weight, preferred_element_type=jnp.float32)
-    value_half = projected[:, :width]
-    gate_half = jax.nn.sigmoid(projected[:, width:])
-    row_keep = keep[:, None]
-    gated = (row_keep * value_half * gate_half).astype(jnp.bfloat16)
-    depthwise = depth_forward(gated, depth_kernel, span)
-    centred_two = depthwise - jnp.mean(depthwise, axis=1, keepdims=True)
-    scale_two = lax.rsqrt(jnp.mean(centred_two * centred_two, axis=1, keepdims=True) + EPSILON)
-    standard_two = centred_two * scale_two
-    active = standard_two * conv_gain.astype(jnp.float32)
-    swish_gate = jax.nn.sigmoid(active)
-    hidden = (active * swish_gate).astype(jnp.bfloat16)
-    mixed = jnp.dot(hidden, down_weight, preferred_element_type=jnp.float32)
-    layer_out = (row_keep * (values + mixed)).astype(jnp.bfloat16)
-    back_out = jnp.where(row_keep > 0, cotangent, jnp.zeros_like(cotangent))
-    back_hidden = lax.dot_general(
-        back_out, down_weight, (((1,), (1,)), ((), ())), preferred_element_type=jnp.float32
-    )
-    back_active = back_hidden * (swish_gate + active * swish_gate * (1.0 - swish_gate))
-    gain_back = back_active * conv_gain.astype(jnp.float32)
-    back_depth = scale_two * (
-        gain_back
-        - jnp.mean(gain_back, axis=1, keepdims=True)
-        - standard_two * jnp.mean(gain_back * standard_two, axis=1, keepdims=True)
-    )
-    back_gated = row_keep * depth_backward(back_depth, depth_kernel, span)
-    back_proj = jnp.concatenate(
-        [back_gated * gate_half, back_gated * value_half * gate_half * (1.0 - gate_half)], axis=1
-    ).astype(jnp.bfloat16)
-    back_normed = lax.dot_general(
-        back_proj, up_weight, (((1,), (1,)), ((), ())), preferred_element_type=jnp.float32
-    )
-    gain_front = back_normed * norm_gain.astype(jnp.float32)
-    back_input = scale_one * (
-        gain_front
-        - jnp.mean(gain_front, axis=1, keepdims=True)
-        - standard * jnp.mean(gain_front * standard, axis=1, keepdims=True)
-    )
-    grad_input = (back_out.astype(jnp.float32) + back_input).astype(jnp.bfloat16)
-    return (layer_out, grad_input, hidden, back_out)
-
-
-def by_panel(rows):
-    return rows.reshape(SPAN, U_DEV, -1).transpose(1, 0, 2).reshape(ROWS, -1)
-
-
-def joined(own, other, dim):
-    order = lax.axis_index("fsdp") == 0
-    first = jnp.where(order, own, other)
-    last = jnp.where(order, other, own)
-    return jnp.concatenate([first, last], axis=dim)
+    swap.start()
+
+    def own_grad(n, carry):
+        grad_own[:, lane_tile(n)] = grad_rows(core, n)
+        return carry
+
+    lax.fori_loop(0, D // N_TILE, own_grad, 0)
+    loads[2].wait()
+    loads[3].wait()
+    swap.wait()
+
+    def add_partner(n, carry):
+        rows = pl.ds(pl.multiple_of(n * 64, 64), 64)
+        part[rows] = (grad_own[rows] + from_partner[rows].astype(F32)).astype(BF)
+        return carry
+
+    lax.fori_loop(0, HALF_D // 64, add_partner, 0)
+
+    def piece(ref, c):
+        return ref.at[
+            pl.ds(pl.multiple_of(c // 2 * SPAN, SPAN), SPAN),
+            pl.ds(pl.multiple_of(c % 2 * HALF_D, HALF_D), HALF_D),
+        ]
+
+    def scatter(step, carry):
+        peer = shifted_peer(me, step)
+        pltpu.make_async_remote_copy(
+            src_ref=piece(part, peer),
+            dst_ref=parts.at[me],
+            send_sem=send_sems.at[0],
+            recv_sem=recv_sems.at[0],
+            device_id=(peer, core),
+            device_id_type=MESH,
+        ).start()
+        return carry
+
+    lax.fori_loop(1, N_DP, scatter, 0)
+    parts[pl.ds(me, 1)] = piece(part, me)[...][None]
+
+    def output(n, carry):
+        mixed = dot(hidden[...], down[:, lane_tile(n)])
+        total = features[:, lane_tile(n)].astype(F32) + mixed
+        total = (keep[:, :1] * total).astype(BF)
+        layer_out[:, lane_tile(n)] = dot(to_panels, total).astype(BF)
+        return carry
+
+    lax.fori_loop(0, D // N_TILE, output, 0)
+
+    def back_hidden(n, carry):
+        rows = down[pl.ds(pl.multiple_of(n * N_TILE, N_TILE), N_TILE)]
+        big[:, lane_tile(n)] = dot_t(back_out[...], rows)
+        return carry
+
+    lax.fori_loop(0, D // N_TILE, back_hidden, 0)
+
+    def back_norm(g, carry):
+        error = big[rows_of(g)] * slope[rows_of(g)]
+        standard = standard_two[rows_of(g)]
+        inner = error - row_mean(error) - standard * row_mean(error * standard)
+        back_depth[rows_of(g, KER // 2)] = stats[2, rows_of(g), :1] * inner
+        return carry
+
+    lax.fori_loop(0, SPAN, back_norm, 0)
+
+    def back_conv(g, carry):
+        summed = None
+        for k in range(KER):
+            tap = depth_kernel[k : k + 1].astype(F32)
+            term = back_depth[rows_of(g, KER - 1 - k)] * tap
+            summed = term if summed is None else summed + term
+        summed = keep[rows_of(g), :1] * summed
+        back_proj[rows_of(g), 0:D] = (summed * gate_a[rows_of(g)]).astype(BF)
+        back_proj[rows_of(g), D : 2 * D] = (summed * gate_b[rows_of(g)]).astype(BF)
+        return carry
+
+    lax.fori_loop(0, SPAN, back_conv, 0)
+
+    def await_all(ref, sem):
+        block = ref.at[pl.ds(0, N_DP - 1)]
+        pltpu.make_async_copy(block, block, sem).wait()
+
+    await_all(parts, recv_sems.at[0])
+    total = parts[0].astype(F32)
+    for k in range(1, N_DP):
+        total = total + parts[k].astype(F32)
+    mine[...] = (total * (1.0 / math.sqrt(ROWS * N_DP * 2))).astype(BF)
+
+    def spread_mine(step, carry):
+        pltpu.make_async_remote_copy(
+            src_ref=mine,
+            dst_ref=shared.at[me],
+            send_sem=send_sems.at[1],
+            recv_sem=recv_sems.at[1],
+            device_id=(shifted_peer(me, step), core),
+            device_id_type=MESH,
+        ).start()
+        return carry
+
+    lax.fori_loop(1, N_DP, spread_mine, 0)
+    shared[pl.ds(me, 1)] = mine[...][None]
+
+    def back_up(n, carry):
+        rows = up[pl.ds(pl.multiple_of(n * N_TILE, N_TILE), N_TILE)]
+        big[:, lane_tile(n)] = dot_t(back_proj[...], rows)
+        return carry
+
+    lax.fori_loop(0, D // N_TILE, back_up, 0)
+
+    def back_first(g, carry):
+        front = big[rows_of(g)] * gain_one
+        scale = stats[1, rows_of(g), :1]
+        standard = (features[rows_of(g)].astype(F32) - stats[0, rows_of(g), :1]) * scale
+        inner = front - row_mean(front) - standard * row_mean(front * standard)
+        normed[rows_of(g)] = (back_out[rows_of(g)].astype(F32) + scale * inner).astype(BF)
+        return carry
+
+    lax.fori_loop(0, SPAN, back_first, 0)
+
+    def reorder(n, carry):
+        grad_input[:, lane_tile(n)] = dot(to_panels, normed[:, lane_tile(n)]).astype(BF)
+        return carry
+
+    lax.fori_loop(0, D // N_TILE, reorder, 0)
+    await_all(shared, recv_sems.at[1])
+
+    def place(c, carry):
+        piece(grad_down, c)[...] = shared[c].astype(F32)
+        return carry
+
+    lax.fori_loop(0, N_DP, place, 0)
+    await_all(parts, send_sems.at[0])
+    await_all(shared, send_sems.at[1])
+
+
+def module(features, keep, cotangent, norm_gain, depth_kernel, conv_gain, ups, downs):
+    rows = (ROWS, D)
+    return pl.pallas_call(
+        module_kernel,
+        out_shape=[
+            jax.ShapeDtypeStruct(rows, BF),
+            jax.ShapeDtypeStruct(rows, BF),
+            jax.ShapeDtypeStruct((HALF_D, D), F32),
+        ],
+        in_specs=[VMEM_SPEC] * 6 + [ANY_SPEC] * 4,
+        out_specs=[VMEM_SPEC] * 3,
+        scratch_shapes=[
+            pltpu.VMEM((D, 2 * D), BF),
+            pltpu.VMEM((D, D), BF),
+            pltpu.VMEM(rows, BF),
+            pltpu.VMEM((3, ROWS, 128), F32),
+            pltpu.VMEM(rows, F32),
+            pltpu.VMEM(rows, F32),
+            pltpu.VMEM((ROWS + 2 * BORDER, D), BF),
+            pltpu.VMEM(rows, F32),
+            pltpu.VMEM(rows, F32),
+            pltpu.VMEM(rows, BF),
+            pltpu.VMEM(rows, BF),
+            pltpu.VMEM((HALF_D, D), F32),
+            pltpu.VMEM((HALF_D, D), BF),
+            pltpu.VMEM((HALF_D, D), BF),
+            pltpu.VMEM((HALF_D, D), BF),
+            pltpu.VMEM((N_DP, SPAN, HALF_D), BF),
+            pltpu.VMEM((SPAN, HALF_D), BF),
+            pltpu.VMEM((N_DP, SPAN, HALF_D), BF),
+            pltpu.VMEM(rows, F32),
+            pltpu.VMEM((ROWS + 2 * BORDER, D), F32),
+            pltpu.VMEM((ROWS, 2 * D), BF),
+            pltpu.SemaphoreType.DMA((4,)),
+            pltpu.SemaphoreType.DMA,
+            pltpu.SemaphoreType.DMA,
+            pltpu.SemaphoreType.DMA((2,)),
+            pltpu.SemaphoreType.DMA((2,)),
+        ],
+        compiler_params=pltpu.CompilerParams(
+            collective_id=1, has_side_effects=True, vmem_limit_bytes=58 << 20
+        ),
+        name="module",
+    )(features, keep, cotangent, norm_gain, depth_kernel, conv_gain, *ups, *downs)
 
 
 def local(
@@ -447,29 +668,16 @@
     big = (linear_weight, up_weight, down_weight)
     windows, keep, band, full, other = exchange(frames[None], target[None], mel_panels, small, big)
     features = subsample(windows, band, *full[1:5], linear_weight, other[0])
-    features = by_panel(features)
-    keep = by_panel(keep)[:, 0]
-    layer_out, grad_input, hidden, back_out = module_pass(
+    return module(
         features,
         keep,
         cotangent,
-        full[5][0],
-        joined(up_weight, other[1], 1),
+        full[5],
         full[6],
-        full[7][0],
-        joined(down_weight, other[2], 0),
-        SPAN,
+        full[7],
+        (up_weight, other[1]),
+        (down_weight, other[2]),
     )
-    local_rows = sent_and_summed(
-        lax.dot_general(
-            hidden, back_out, (((0,), (0,)), ((), ())), preferred_element_type=jnp.float32
-        ).astype(jnp.bfloat16),
-        "fsdp",
-        0,
-    )
-    summed = lax.psum(local_rows, "dp")
-    grad_down = summed / jnp.sqrt(jnp.float32(ROWS * N_DP * 2))
-    return (layer_out, grad_input, grad_down)
 
 
 def solution(mesh):

time: 254 us -> 146 us (0.57)
  waiting for transfers between devices: 113 us -> 0 us
  Pallas kernels: 65.1 us -> 123 us
  other arithmetic: 23.2 us -> 0 us
  between operations: 14.4 us -> 0.7 us
  matrix products: 10.7 us -> 0 us
  blocking collectives: 5.42 us -> 0 us
    psum x1 -> x0, waiting for transfers between devices: 113 us -> none  [local(): summed = lax.psum(local_rows, 'dp')]
    pallas_call x0 -> x1, Pallas kernels: none -> 57.8 us  [module(): pl.pallas_call(module_kernel, out_shape=[jax.ShapeDtypeStruct(rows, BF),...]
    dot_general x5 -> x0, matrix products: 10.7 us -> none  [the longest x1 2.65 us: module_pass(): lax.dot_general(back_proj, up_weight, (((1,), (1,)), ((), ())), preferred...]
    reduce_sum x5 -> x0, other arithmetic: 8.02 us -> none  [the longest x1 2.73 us: module_pass(): centred_two = depthwise - jnp.mean(depthwise, axis=1, keepdims=True)]
    all_to_all x1 -> x0, blocking collectives: 5.42 us -> none  [sent_and_summed(): tiles = lax.all_to_all(in_blocks(value, dim, size), axis, 0, 0, tiled=True)]
    convert_element_type x5 -> x0, other arithmetic: 4.5 us -> none  [the longest x1 1.97 us: module_pass(): (back_out.astype(jnp.float32) + back_input).astype(jnp.bfloat16)]
    select_n x2 -> x0, other arithmetic: 3.4 us -> none  [joined(): first = jnp.where(order, own, other)]
    div x6 -> x0, other arithmetic: 3.24 us -> none  [the longest x1 3.22 us: local(): grad_down = summed / jnp.sqrt(jnp.float32(ROWS * N_DP * 2))]
  transfers between devices with their start and end apart: 1 -> 0, of which waited for: 1 -> 0; matrix products, arithmetic and copies ran while one was open for 5% -> 0% of each run, Pallas kernels for 0% -> 0%
where the time goes in v2:
time: 146 us; the launch traced here: 145 us
  Pallas kernels  123 us (84%)
  local copies, waits for them, and re-layouts  21.3 us (15%)
    pallas_call x1, Pallas kernels, module(): pl.pallas_call(module_kernel, out_shape=[jax.ShapeDtypeStruct(rows, BF),...  57.8 us
    pallas_call x1, Pallas kernels, exchange(): pl.pallas_call(exchange_kernel, out_shape=shapes, in_specs=[VMEM_SPEC] *...  35.2 us
    pallas_call x1, Pallas kernels, subsample(): pl.pallas_call(subsample_kernel, out_shape=jax.ShapeDtypeStruct((ROWS, D)...  29.8 us
    unnamed x47, local copies, waits for them, and re-layouts  19.9 us

profile of v2, /device:TPU:0, one launch (start us, length us, event | category | flops | bytes accessed | tf_op | source)
XLA Modules:
  0.0 144.9 jit_solution(11735249646102166064)
XLA Ops:
  0.6 0.7 broadcast_in_dim.14.refs_8_
  1.3 0.7 broadcast_in_dim.15.refs_10_
  2.0 1.2 copy-done
  3.2 1.3 copy-done.1
  4.5 0.8 copy-done.7
  5.4 0.8 copy-done.8
  6.2 0.7 copy-done.10
  6.9 0.7 copy-done.15
  7.6 0.7 copy-done.16
  8.3 0.7 copy-done.17
  9.0 0.7 copy-done.18
  9.7 0.7 copy-done.19
  10.3 35.2 %exchange.1 = (bf16[2048,256]{1,0:T(8,128)(2,1)S(1)}, f32[512,128]{1,0:T(8,128)S(1)}, bf16[256,10240]{1,0:T(8,128)(2,1)}, bf16[9,256]{1,0:T(8,128)(2,1)}, bf16[9...) custom-call(s32[1,64]{1,0:T(1,128)S(1)} %bitcast.2, ...), custom_call_target="tpu_custom_call" | custom-call | tf_op jit(solution)/shard_map/exchange/pallas_call | solution.py:196
  45.5 0.0 copy-start.2
  45.6 1.0 copy-done.2
  46.5 1.0 copy-done.3
  47.5 0.7 copy-done.4
  48.2 0.6 copy-done.5
  48.8 0.6 copy-done.6
  49.5 0.6 copy-done.9
  50.1 0.6 copy-done.11
  50.7 0.6 copy-done.12
  51.3 0.6 copy-done.13
  51.9 0.6 copy-done.14
  52.5 29.8 %subsample.1.features = bf16[512,1024]{1,0:T(8,128)(2,1)} custom-call(bf16[2048,256]{1,0:T(8,128)(2,1)} %copy-done.3, bf16[256,10240]{1,0:T(8,128)(2,1)} %get-tuple-element.17.band, bf16[9,256]{1,0:T(8,128)(2,1)} %copy-done.11, bf16[256,256]{1,0:T(8,128)(2,1)} %copy-done.5, bf16[9,256]{1,0:T(8,128)(2,1)} %copy-done.12, bf16[256,256]{1,0:T(8,128)(2,1)} %copy-done.6, ...), custom_call_target="tpu_custom_call" | custom-call | tf_op jit(solution)/shard_map/subsample/pallas_call | solution.py:303
  82.3 57.8 %module.1 = (bf16[512,1024]{1,0:T(8,128)(2,1)}, bf16[512,1024]{1,0:T(8,128)(2,1)}, f32[512,1024]{1,0:T(8,128)}) custom-call(bf16[512,1024]{1,0:T(8,128)(2,1)} %subsample.1.features, f32[512,128]{1,0:T(8,128)} %copy-done.4, bf16[512,1024]{1,0:T(8,128)(2,1)} %cotangent.1, bf16[1,1024]{1,0:T(2,128)(2,1)} %copy-done.13, bf16[9,1024]{1,0:T(8,128)(2,1)} %copy-done.9, ...), custom_call_target="tpu_custom_call" | custom-call | tf_op jit(solution)/shard_map/module/pallas_call | solution.py:597
  140.2 0.0 copy-start.21
  140.2 0.0 copy-start.20
  140.2 2.4 %copy.21 = bf16[512,1024]{1,0:T(8,128)(2,1)} copy(bf16[512,1024]{1,0:T(8,128)(2,1)} %get-tuple-element.32) | data formatting | bytes 2097152
  142.6 0.0 copy-done.21
  142.6 1.0 copy.22
  143.6 1.3 copy.23
  (20 shorter events, 0.0 us)
Async XLA Ops:
  2.0 1.2 copy-start
  3.2 1.3 copy-start.1
  4.5 0.8 copy-start.7
  5.4 0.8 copy-start.8
  6.2 0.7 copy-start.10
  6.9 0.7 copy-start.15
  7.6 0.7 copy-start.16
  8.3 0.7 copy-start.17
  9.0 0.7 copy-start.18
  9.7 0.7 copy-start.19
  45.5 1.0 copy-start.2
  46.5 1.0 copy-start.3
  47.5 0.7 copy-start.4
  48.2 0.7 copy-start.5
  48.8 0.7 copy-start.6
  49.5 0.6 copy-start.9
  50.1 0.6 copy-start.11
  50.7 0.6 copy-start.12
  51.3 0.6 copy-start.13
  51.9 0.6 copy-start.14
  140.2 2.4 %copy-start.21 = (bf16[512,1024]{1,0:T(8,128)(2,1)S(1)}, bf16[512,1024]{1,0:T(8,128)(2,1)}, u32[]{:S(2)}) copy-start(bf16[512,1024]{1,0:T(8,128)(2,1)} %get-tuple-element.33) | copy-start | bytes 3145732
  140.2 3.4 %copy-start.20 = (f32[512,1024]{1,0:T(8,128)S(1)}, f32[512,1024]{1,0:T(8,128)}, u32[]{:S(2)}) copy-start(f32[512,1024]{1,0:T(8,128)} %get-tuple-element.34) | copy-start | bytes 6291460

commit v3 on v2

--- a/solution.py
+++ b/solution.py
@@ -211,7 +211,7 @@
             pltpu.SemaphoreType.DMA,
         ],
         compiler_params=pltpu.CompilerParams(
-            collective_id=0, has_side_effects=True, vmem_limit_bytes=48 << 20
+            collective_id=0, has_side_effects=True, vmem_limit_bytes=67043328
         ),
         name="exchange",
     )(frames, target, mel, *small, *big)
@@ -314,7 +314,7 @@
             pltpu.VMEM((10 * CH, D), BF),
             pltpu.SemaphoreType.DMA((2,)),
         ],
-        compiler_params=pltpu.CompilerParams(vmem_limit_bytes=56 << 20),
+        compiler_params=pltpu.CompilerParams(vmem_limit_bytes=67043328),
         name="subsample",
     )(windows, band, depth_a, point_a, depth_b, point_b, linear_own, linear_other)
 
@@ -632,7 +632,7 @@
             pltpu.SemaphoreType.DMA((2,)),
         ],
         compiler_params=pltpu.CompilerParams(
-            collective_id=1, has_side_effects=True, vmem_limit_bytes=58 << 20
+            collective_id=1, has_side_effects=True, vmem_limit_bytes=67043328
         ),
         name="module",
     )(features, keep, cotangent, norm_gain, depth_kernel, conv_gain, *ups, *downs)

time: 146 us -> 134 us (0.918)
  local copies, waits for them, and re-layouts: 21.3 us -> 7.23 us
  Pallas kernels: 123 us -> 125 us
    unnamed x47 -> x7, local copies, waits for them, and re-layouts: 19.9 us -> 4.71 us
    pallas_call x1, Pallas kernels: 35.2 us -> 37.2 us  [exchange(): pl.pallas_call(exchange_kernel, out_shape=shapes, in_specs=[VMEM_SPEC] *...]
where the time goes in v3:
time: 134 us; the launch traced here: 133 us
  Pallas kernels  125 us (93%)
  local copies, waits for them, and re-layouts  7.23 us (5%)
    pallas_call x1, Pallas kernels, module(): pl.pallas_call(module_kernel, out_shape=[jax.ShapeDtypeStruct(rows, BF),...  58 us
    pallas_call x1, Pallas kernels, exchange(): pl.pallas_call(exchange_kernel, out_shape=shapes, in_specs=[VMEM_SPEC] *...  37.2 us
    pallas_call x1, Pallas kernels, subsample(): pl.pallas_call(subsample_kernel, out_shape=jax.ShapeDtypeStruct((ROWS, D)...  29.8 us
    unnamed x7, local copies, waits for them, and re-layouts  4.71 us

profile of v3, /device:TPU:0, one launch (start us, length us, event | category | flops | bytes accessed | tf_op | source)
XLA Modules:
  0.0 133.0 jit_solution(3762855869958462092)
XLA Ops:
  0.6 1.3 broadcast_in_dim.14.refs_8_
  1.9 1.3 broadcast_in_dim.15.refs_10_
  3.1 37.2 %exchange.1 = (bf16[2048,256]{1,0:T(8,128)(2,1)}, f32[512,128]{1,0:T(8,128)}, bf16[256,10240]{1,0:T(8,128)(2,1)}, bf16[9,256]{1,0:T(8,128)(2,1)}, bf16[9,256]{1,...) custom-call(s32[1,64]{1,0:T(1,128)} %bitcast.2, ...), custom_call_target="tpu_custom_call" | custom-call | tf_op jit(solution)/shard_map/exchange/pallas_call | solution.py:196
  40.4 29.8 %subsample.1.features = bf16[512,1024]{1,0:T(8,128)(2,1)} custom-call(bf16[2048,256]{1,0:T(8,128)(2,1)} %get-tuple-element.16.windows, bf16[256,10240]{1,0:T(8,128)(2,1)} %get-tuple-element.17.band, bf16[9,256]{1,0:T(8,128)(2,1)} %get-tuple-element.18.depth_a, bf16[256,256]{1,0:T(8,128)(2,1)} %get-tuple-element.19.point_a, ...), custom_call_target="tpu_custom_call" | custom-call | tf_op jit(solution)/shard_map/subsample/pallas_call | solution.py:303
  70.3 58.0 %module.1 = (bf16[512,1024]{1,0:T(8,128)(2,1)}, bf16[512,1024]{1,0:T(8,128)(2,1)}, f32[512,1024]{1,0:T(8,128)}) custom-call(bf16[512,1024]{1,0:T(8,128)(2,1)} %subsample.1.features, f32[512,128]{1,0:T(8,128)} %get-tuple-element.23.keep, bf16[512,1024]{1,0:T(8,128)(2,1)} %cotangent.1, bf16[1,1024]{1,0:T(2,128)(2,1)} %get-tuple-element.24.norm_gain, ...), custom_call_target="tpu_custom_call" | custom-call | tf_op jit(solution)/shard_map/module/pallas_call | solution.py:597
  128.2 0.0 copy-start.1
  128.2 0.0 copy-start
  128.2 2.4 %copy.21 = bf16[512,1024]{1,0:T(8,128)(2,1)} copy(bf16[512,1024]{1,0:T(8,128)(2,1)} %get-tuple-element.32) | data formatting | bytes 2097152
  130.7 0.0 copy-done.1
  130.7 1.0 copy.22
  131.6 0.0 copy-done
  131.6 1.3 copy.23
Async XLA Ops:
  128.2 2.4 %copy-start.1 = (bf16[512,1024]{1,0:T(8,128)(2,1)S(1)}, bf16[512,1024]{1,0:T(8,128)(2,1)}, u32[]{:S(2)}) copy-start(bf16[512,1024]{1,0:T(8,128)(2,1)} %get-tuple-element.33) | copy-start | bytes 3145732
  128.2 3.4 %copy-start = (f32[512,1024]{1,0:T(8,128)S(1)}, f32[512,1024]{1,0:T(8,128)}, u32[]{:S(2)}) copy-start(f32[512,1024]{1,0:T(8,128)} %get-tuple-element.34) | copy-start | bytes 6291460

commit v4 on v3

--- a/solution.py
+++ b/solution.py
@@ -42,20 +42,20 @@
     return z * 16 + y * 4 + x
 
 
-N_SMALL = 8
+N_SMALL = 7
 N_BIG = 3
 
 
 def exchange_kernel(*refs):
     frames, target, mel = refs[:3]
     small = refs[3 : 3 + N_SMALL]
-    big = refs[11:14]
-    windows, keep_out, band_out = refs[14:17]
-    small_full = refs[17 : 17 + N_SMALL]
-    big_other = refs[25:28]
-    flat, outgoing, incoming = refs[28:31]
-    small_other = refs[31 : 31 + N_SMALL]
-    small_send, small_recv, big_send, big_recv, send_sem, recv_sem = refs[39:]
+    big = refs[10:13]
+    windows, keep_out, band_out = refs[13:16]
+    small_full = refs[16 : 16 + N_SMALL]
+    big_other = refs[23:26]
+    flat, outgoing, incoming, band_in = refs[26:30]
+    small_other = refs[30 : 30 + N_SMALL]
+    small_send, small_recv, big_send, big_recv, send_sem, recv_sem, band_sem = refs[37:]
 
     me = lax.axis_index("dp")
     core = lax.axis_index("fsdp")
@@ -137,10 +137,12 @@
         b = base + (tap % 3) - 1
         hit = (base == 2 * f) & (b >= 0) & (b < MELS)
         column = dot(jnp.where(hit, 1.0, 0.0).astype(BF), taps)
-        band_out[:, pl.ds(pl.multiple_of(f * CH, CH), CH)] = column.astype(BF)
+        band_in[:, pl.ds(pl.multiple_of(f * CH, CH), CH)] = column.astype(BF)
         return carry
 
     lax.fori_loop(0, MELS // 2, band, 0)
+    band_copy = pltpu.make_async_copy(band_in, band_out, band_sem)
+    band_copy.start()
 
     sent = outgoing.at[pl.ds(0, N_DP - 1)]
     got = incoming.at[pl.ds(0, N_DP - 1)]
@@ -182,6 +184,7 @@
     pltpu.make_async_copy(sent, sent, send_sem).wait()
     for k in range(N_SMALL, N_SMALL + N_BIG):
         partner[k].wait()
+    band_copy.wait()
 
 
 def exchange(frames, target, mel, small, big):
@@ -197,16 +200,18 @@
         exchange_kernel,
         out_shape=shapes,
         in_specs=[VMEM_SPEC] * (3 + N_SMALL) + [ANY_SPEC] * N_BIG,
-        out_specs=[VMEM_SPEC] * (3 + N_SMALL) + [ANY_SPEC] * N_BIG,
+        out_specs=[VMEM_SPEC] * 2 + [ANY_SPEC] + [VMEM_SPEC] * N_SMALL + [ANY_SPEC] * N_BIG,
         scratch_shapes=[
             pltpu.VMEM((GROUP // 128, N_DP * SPAN, 128), F32),
             pltpu.VMEM((N_DP, SPAN, GROUP), BF),
             pltpu.VMEM((N_DP, SPAN, GROUP), BF),
+            pltpu.VMEM((256, MELS // 2 * CH), BF),
             *[pltpu.VMEM(a.shape, BF) for a in small],
             pltpu.SemaphoreType.DMA((N_SMALL,)),
             pltpu.SemaphoreType.DMA((N_SMALL,)),
             pltpu.SemaphoreType.DMA((N_BIG,)),
             pltpu.SemaphoreType.DMA((N_BIG,)),
+            pltpu.SemaphoreType.DMA,
             pltpu.SemaphoreType.DMA,
             pltpu.SemaphoreType.DMA,
         ],
@@ -232,51 +237,67 @@
 
 
 def subsample_kernel(
-    windows, band, depth_a, point_a, depth_b, point_b, linear_own, linear_other, out,
-    first, spread_a, second, spread_b, fourth, linear, sems
+    windows, band_in, depth_a, point_a, depth_b, point_b, linear_own, linear_other, out,
+    band, first, spread_a, second, spread_b, fourth, linear, sems
 ):
     core = lax.axis_index("fsdp")
     width = D // 2
+
+    def half(which):
+        return linear.at[:, pl.ds(pl.multiple_of(which * width, width), width)]
+
+    early, late = pl.ds(0, 4 * CH), pl.ds(4 * CH, MELS // 2 * CH - 4 * CH)
     loads = [
-        pltpu.make_async_copy(
-            linear_own, linear.at[:, pl.ds(pl.multiple_of(core * width, width), width)], sems.at[0]
-        ),
-        pltpu.make_async_copy(
-            linear_other,
-            linear.at[:, pl.ds(pl.multiple_of((1 - core) * width, width), width)],
-            sems.at[1],
-        ),
+        pltpu.make_async_copy(band_in.at[:, early], band.at[:, early], sems.at[0]),
+        pltpu.make_async_copy(band_in.at[:, late], band.at[:, late], sems.at[1]),
+        pltpu.make_async_copy(linear_own, half(core), sems.at[2]),
+        pltpu.make_async_copy(linear_other, half(1 - core), sems.at[3]),
     ]
     for copy in loads:
         copy.start()
-    first[:, 0] = jnp.zeros((4, PAD + ROWS, CH), BF)
+    inner = slice(PAD, PAD + ROWS)
+    first[0, :, 0] = jnp.zeros((4, PAD + ROWS, CH), BF)
     second[:, 0] = jnp.zeros((2, PAD + ROWS, CH), BF)
     for col in range(1, 5):
-        first[3, col, 0:PAD] = jnp.zeros((PAD, CH), BF)
+        for b in range(2):
+            first[b, 3, col, 0:PAD] = jnp.zeros((PAD, CH), BF)
     for col in range(1, 3):
         second[1, col, 0:PAD] = jnp.zeros((PAD, CH), BF)
     taps_a = [jnp.broadcast_to(depth_a[k : k + 1], (CHUNK, CH)) for k in range(9)]
     taps_b = [jnp.broadcast_to(depth_b[k : k + 1], (CHUNK, CH)) for k in range(9)]
 
-    def step(n, carry):
-        for t in range(4):
-            x = windows[t * ROWS : (t + 1) * ROWS]
-            for f in range(4):
-                w = band[:, pl.ds(pl.multiple_of(n * 4 * CH + f * CH, CH), CH)]
-                first[t, 1 + f, PAD : PAD + ROWS] = jnp.maximum(dot(x, w), 0.0).astype(BF)
-        for t2 in range(2):
-            for f2 in range(2):
-
-                def load(i, j, r):
-                    t = 2 * t2 + i - 1
-                    if t < 0:
-                        return first[3, 2 * f2 + j, r : r + CHUNK]
-                    return first[t, 2 * f2 + j, PAD + r : PAD + r + CHUNK]
-
-                for r in range(0, ROWS, CHUNK):
-                    spread_a[r : r + CHUNK] = depth_rows(load, taps_a, r)
-                mapped = dot(spread_a[...], point_a[...])
-                second[t2, 1 + f2, PAD : PAD + ROWS] = jnp.maximum(mapped, 0.0).astype(BF)
+    def relu(x):
+        return jnp.maximum(x.astype(BF), 0)
+
+    def columns(n, b, t, f):
+        w = band[:, pl.ds(pl.multiple_of(n * 4 * CH + f * CH, CH), CH)]
+        first[b, t, 1 + f, inner] = relu(dot(windows[t * ROWS : (t + 1) * ROWS], w))
+
+    jobs = [(t, f) for f in range(4) for t in range(4)]
+
+    def step(n, b):
+        ahead = jnp.minimum(n + 1, 9)
+        for t in range(3):
+            first[1 - b, t, 0, inner] = first[b, t, 4, inner]
+        first[1 - b, 3, 0] = first[b, 3, 4]
+        at = 0
+        for q in range(4):
+            t2, f2 = q // 2, q % 2
+            for t, f in jobs[at : at + 3]:
+                columns(ahead, 1 - b, t, f)
+            at += 3
+
+            def load(i, j, r):
+                t = 2 * t2 + i - 1
+                if t < 0:
+                    return first[b, 3, 2 * f2 + j, r : r + CHUNK]
+                return first[b, t, 2 * f2 + j, PAD + r : PAD + r + CHUNK]
+
+            for r in range(0, ROWS, CHUNK):
+                spread_a[q, r : r + CHUNK] = depth_rows(load, taps_a, r)
+            second[t2, 1 + f2, inner] = relu(dot(spread_a[q], point_a[...]))
+        for t, f in jobs[at:]:
+            columns(ahead, 1 - b, t, f)
 
         def load_b(i, j, r):
             if i == 0:
@@ -285,17 +306,24 @@
 
         for r in range(0, ROWS, CHUNK):
             spread_b[r : r + CHUNK] = depth_rows(load_b, taps_b, r)
-        mapped = dot(spread_b[...], point_b[...])
-        fourth[:, pl.ds(pl.multiple_of(n * CH, CH), CH)] = jnp.maximum(mapped, 0.0).astype(BF)
-        for t in range(4):
-            first[t, 0] = first[t, 4]
+        mapped = relu(dot(spread_b[...], point_b[...]))
+        fourth[:, pl.ds(pl.multiple_of(n * CH, CH), CH)] = mapped
         for t2 in range(2):
             second[t2, 0] = second[t2, 2]
-        return carry
-
-    lax.fori_loop(0, 10, step, 0)
-    for copy in loads:
-        copy.wait()
+
+    loads[0].wait()
+    for t, f in jobs:
+        columns(0, 0, t, f)
+    loads[1].wait()
+
+    def two_steps(m, carry):
+        step(2 * m, 0)
+        step(2 * m + 1, 1)
+        return carry
+
+    lax.fori_loop(0, 5, two_steps, 0)
+    loads[2].wait()
+    loads[3].wait()
     out[...] = dot(fourth[...], linear[...]).astype(BF)
 
 
@@ -303,16 +331,17 @@
     return pl.pallas_call(
         subsample_kernel,
         out_shape=jax.ShapeDtypeStruct((ROWS, D), BF),
-        in_specs=[VMEM_SPEC] * 6 + [ANY_SPEC] * 2,
+        in_specs=[VMEM_SPEC, ANY_SPEC] + [VMEM_SPEC] * 4 + [ANY_SPEC] * 2,
         out_specs=VMEM_SPEC,
         scratch_shapes=[
-            pltpu.VMEM((4, 5, PAD + ROWS, CH), BF),
-            pltpu.VMEM((ROWS, CH), BF),
+            pltpu.VMEM((256, MELS // 2 * CH), BF),
+            pltpu.VMEM((2, 4, 5, PAD + ROWS, CH), BF),
+            pltpu.VMEM((4, ROWS, CH), BF),
             pltpu.VMEM((2, 3, PAD + ROWS, CH), BF),
             pltpu.VMEM((ROWS, CH), BF),
             pltpu.VMEM((ROWS, 10 * CH), BF),
             pltpu.VMEM((10 * CH, D), BF),
-            pltpu.SemaphoreType.DMA((2,)),
+            pltpu.SemaphoreType.DMA((4,)),
         ],
         compiler_params=pltpu.CompilerParams(vmem_limit_bytes=67043328),
         name="subsample",
@@ -341,13 +370,37 @@
     return pl.ds(pl.multiple_of(start + n * N_TILE, N_TILE), N_TILE)
 
 
+LANES = ((0, 384), (384, 384), (768, 256))
+LINE = 128
+OWN = 8
+
+
+def line_of(me, c):
+    x, y, z = me % 4, me // 4 % 4, me // 16
+    return ((x, z * 4 + y), (y, z * 4 + x), (z, y * 4 + x))[c]
+
+
+def device_at(c, a, p):
+    if c == 0:
+        return p // 4 * 16 + p % 4 * 4 + a
+    if c == 1:
+        return p // 4 * 16 + a * 4 + p % 4
+    return a * 16 + p
+
+
+def plane_shift(p, step):
+    return (p // 4 + step // 4) % 4 * 4 + (p + step) % 4
+
+
 def module_kernel(
-    features, keep, cotangent, norm_gain, depth_kernel, conv_gain,
+    features, keep, cotangent, gains, depth_kernel,
     up_own, up_other, down_own, down_other,
     layer_out, grad_input, grad_down,
     up, down, normed, stats, gate_a, gate_b, gated, standard_two, slope, hidden, back_out,
-    grad_own, to_partner, from_partner, part, parts, mine, shared, big, back_depth, back_proj,
-    load_sems, partner_send, partner_recv, send_sems, recv_sems,
+    grad_own, to_partner, from_partner, part, shared, big, back_depth, back_proj,
+    line_a, line_b, line_c, mid_a, mid_b, mid_c, wide_a, wide_b, wide_c,
+    plane_a, plane_b, plane_c, mine_a, mine_b, mine_c,
+    load_sems, partner_send, partner_recv, send_sems, recv_sems, own_sems,
 ):
     me = lax.axis_index("dp")
     core = lax.axis_index("fsdp")
@@ -378,8 +431,8 @@
     def rows_of(g, shift=0):
         return pl.ds(pl.multiple_of((g + shift) * U_DEV, U_DEV), U_DEV)
 
-    gain_one = norm_gain[...].astype(F32)
-    gain_two = conv_gain[...].astype(F32)
+    gain_one = gains[0:1].astype(F32)
+    gain_two = gains[1:2].astype(F32)
 
     def norm_rows(g, carry):
         values = features[rows_of(g)].astype(F32)
@@ -476,26 +529,93 @@
 
     lax.fori_loop(0, HALF_D // 64, add_partner, 0)
 
-    def piece(ref, c):
-        return ref.at[
-            pl.ds(pl.multiple_of(c // 2 * SPAN, SPAN), SPAN),
-            pl.ds(pl.multiple_of(c % 2 * HALF_D, HALF_D), HALF_D),
-        ]
-
-    def scatter(step, carry):
-        peer = shifted_peer(me, step)
+    line_in = (line_a, line_b, line_c)
+    mid = (mid_a, mid_b, mid_c)
+    wide = (wide_a, wide_b, wide_c)
+    plane_in = (plane_a, plane_b, plane_c)
+    mine = (mine_a, mine_b, mine_c)
+
+    def line_rows(a):
+        return pl.ds(pl.multiple_of(a * LINE, LINE), LINE)
+
+    def own_rows(a, p):
+        return pl.ds(pl.multiple_of(a * LINE + p * OWN, OWN), OWN)
+
+    def push(stage, c, src, dst, peer):
         pltpu.make_async_remote_copy(
-            src_ref=piece(part, peer),
-            dst_ref=parts.at[me],
-            send_sem=send_sems.at[0],
-            recv_sem=recv_sems.at[0],
+            src_ref=src,
+            dst_ref=dst,
+            send_sem=send_sems.at[stage, c],
+            recv_sem=recv_sems.at[stage, c],
             device_id=(peer, core),
             device_id_type=MESH,
         ).start()
-        return carry
-
-    lax.fori_loop(1, N_DP, scatter, 0)
-    parts[pl.ds(me, 1)] = piece(part, me)[...][None]
+
+    def await_block(block, sem):
+        pltpu.make_async_copy(block, block, sem).wait()
+
+    def reduce_lines():
+        for c, (at, width) in enumerate(LANES):
+            a, p = line_of(me, c)
+            for step in range(1, 4):
+                to = (a + step) % 4
+                push(
+                    0, c, part.at[line_rows(to), at : at + width], line_in[c].at[step - 1],
+                    device_at(c, to, p),
+                )
+
+    def reduce_planes():
+        for c, (at, width) in enumerate(LANES):
+            a, p = line_of(me, c)
+            await_block(line_in[c], recv_sems.at[0, c])
+            total = part[line_rows(a), at : at + width].astype(F32)
+            for k in range(3):
+                total = total + line_in[c][k].astype(F32)
+            wide[c][...] = total
+            mid[c][...] = total.astype(BF)
+        for c, (at, width) in enumerate(LANES):
+            a, p = line_of(me, c)
+
+            def send(step, carry, c=c, a=a, p=p):
+                to = plane_shift(p, step)
+                push(
+                    1, c, mid[c].at[pl.ds(pl.multiple_of(to * OWN, OWN), OWN)],
+                    plane_in[c].at[step - 1], device_at(c, a, to),
+                )
+                return carry
+
+            lax.fori_loop(1, 16, send, 0)
+
+    def gather_planes():
+        for c, (at, width) in enumerate(LANES):
+            a, p = line_of(me, c)
+            await_block(plane_in[c], recv_sems.at[1, c])
+            total = wide[c][pl.ds(pl.multiple_of(p * OWN, OWN), OWN)]
+            for k in range(15):
+                total = total + plane_in[c][k].astype(F32)
+            mine[c][...] = (total * (1.0 / math.sqrt(ROWS * N_DP * 2))).astype(BF)
+        for c, (at, width) in enumerate(LANES):
+            a, p = line_of(me, c)
+            spot = shared.at[own_rows(a, p), at : at + width]
+            pltpu.make_async_copy(mine[c], spot, own_sems.at[c]).start()
+
+            def send(step, carry, c=c, a=a, p=p, spot=spot):
+                push(2, c, mine[c], spot, device_at(c, a, plane_shift(p, step)))
+                return carry
+
+            lax.fori_loop(1, 16, send, 0)
+
+    def gather_lines():
+        for c, (at, width) in enumerate(LANES):
+            a, p = line_of(me, c)
+            spot = shared.at[own_rows(a, p), at : at + width]
+            pltpu.make_async_copy(mine[c], spot, own_sems.at[c]).wait()
+            await_block(plane_in[c], recv_sems.at[2, c])
+            block = shared.at[line_rows(a), at : at + width]
+            for step in range(1, 4):
+                push(3, c, block, block, device_at(c, (a + step) % 4, p))
+
+    reduce_lines()
 
     def output(n, carry):
         mixed = dot(hidden[...], down[:, lane_tile(n)])
@@ -521,6 +641,8 @@
         return carry
 
     lax.fori_loop(0, SPAN, back_norm, 0)
+
+    reduce_planes()
 
     def back_conv(g, carry):
         summed = None
@@ -535,29 +657,7 @@
 
     lax.fori_loop(0, SPAN, back_conv, 0)
 
-    def await_all(ref, sem):
-        block = ref.at[pl.ds(0, N_DP - 1)]
-        pltpu.make_async_copy(block, block, sem).wait()
-
-    await_all(parts, recv_sems.at[0])
-    total = parts[0].astype(F32)
-    for k in range(1, N_DP):
-        total = total + parts[k].astype(F32)
-    mine[...] = (total * (1.0 / math.sqrt(ROWS * N_DP * 2))).astype(BF)
-
-    def spread_mine(step, carry):
-        pltpu.make_async_remote_copy(
-            src_ref=mine,
-            dst_ref=shared.at[me],
-            send_sem=send_sems.at[1],
-            recv_sem=recv_sems.at[1],
-            device_id=(shifted_peer(me, step), core),
-            device_id_type=MESH,
-        ).start()
-        return carry
-
-    lax.fori_loop(1, N_DP, spread_mine, 0)
-    shared[pl.ds(me, 1)] = mine[...][None]
+    gather_planes()
 
     def back_up(n, carry):
         rows = up[pl.ds(pl.multiple_of(n * N_TILE, N_TILE), N_TILE)]
@@ -565,6 +665,8 @@
         return carry
 
     lax.fori_loop(0, D // N_TILE, back_up, 0)
+
+    gather_lines()
 
     def back_first(g, carry):
         front = big[rows_of(g)] * gain_one
@@ -581,18 +683,23 @@
         return carry
 
     lax.fori_loop(0, D // N_TILE, reorder, 0)
-    await_all(shared, recv_sems.at[1])
-
-    def place(c, carry):
-        piece(grad_down, c)[...] = shared[c].astype(F32)
-        return carry
-
-    lax.fori_loop(0, N_DP, place, 0)
-    await_all(parts, send_sems.at[0])
-    await_all(shared, send_sems.at[1])
-
-
-def module(features, keep, cotangent, norm_gain, depth_kernel, conv_gain, ups, downs):
+    for c in range(3):
+        await_block(line_in[c], recv_sems.at[3, c])
+
+    def place(n, carry):
+        rows = pl.ds(pl.multiple_of(n * 64, 64), 64)
+        grad_down[rows] = shared[rows].astype(F32)
+        return carry
+
+    lax.fori_loop(0, HALF_D // 64, place, 0)
+    for c in range(3):
+        await_block(line_in[c], send_sems.at[0, c])
+        await_block(plane_in[c], send_sems.at[1, c])
+        await_block(plane_in[c], send_sems.at[2, c])
+        await_block(line_in[c], send_sems.at[3, c])
+
+
+def module(features, keep, cotangent, gains, depth_kernel, ups, downs):
     rows = (ROWS, D)
     return pl.pallas_call(
         module_kernel,
@@ -601,7 +708,7 @@
             jax.ShapeDtypeStruct(rows, BF),
             jax.ShapeDtypeStruct((HALF_D, D), F32),
         ],
-        in_specs=[VMEM_SPEC] * 6 + [ANY_SPEC] * 4,
+        in_specs=[VMEM_SPEC] * 5 + [ANY_SPEC] * 4,
         out_specs=[VMEM_SPEC] * 3,
         scratch_shapes=[
             pltpu.VMEM((D, 2 * D), BF),
@@ -619,23 +726,27 @@
             pltpu.VMEM((HALF_D, D), BF),
             pltpu.VMEM((HALF_D, D), BF),
             pltpu.VMEM((HALF_D, D), BF),
-            pltpu.VMEM((N_DP, SPAN, HALF_D), BF),
-            pltpu.VMEM((SPAN, HALF_D), BF),
-            pltpu.VMEM((N_DP, SPAN, HALF_D), BF),
+            pltpu.VMEM((HALF_D, D), BF),
             pltpu.VMEM(rows, F32),
             pltpu.VMEM((ROWS + 2 * BORDER, D), F32),
             pltpu.VMEM((ROWS, 2 * D), BF),
+            *[pltpu.VMEM((3, LINE, width), BF) for _, width in LANES],
+            *[pltpu.VMEM((LINE, width), BF) for _, width in LANES],
+            *[pltpu.VMEM((LINE, width), F32) for _, width in LANES],
+            *[pltpu.VMEM((15, OWN, width), BF) for _, width in LANES],
+            *[pltpu.VMEM((OWN, width), BF) for _, width in LANES],
             pltpu.SemaphoreType.DMA((4,)),
             pltpu.SemaphoreType.DMA,
             pltpu.SemaphoreType.DMA,
-            pltpu.SemaphoreType.DMA((2,)),
-            pltpu.SemaphoreType.DMA((2,)),
+            pltpu.SemaphoreType.DMA((4, 3)),
+            pltpu.SemaphoreType.DMA((4, 3)),
+            pltpu.SemaphoreType.DMA((3,)),
         ],
         compiler_params=pltpu.CompilerParams(
             collective_id=1, has_side_effects=True, vmem_limit_bytes=67043328
         ),
         name="module",
-    )(features, keep, cotangent, norm_gain, depth_kernel, conv_gain, *ups, *downs)
+    )(features, keep, cotangent, gains, depth_kernel, *ups, *downs)
 
 
 def local(
@@ -661,9 +772,8 @@
         point_a,
         depth_b,
         point_b,
-        norm_gain[None],
+        jnp.stack([norm_gain, conv_gain]),
         depth_kernel,
-        conv_gain[None],
     )
     big = (linear_weight, up_weight, down_weight)
     windows, keep, band, full, other = exchange(frames[None], target[None], mel_panels, small, big)
@@ -674,7 +784,6 @@
         cotangent,
         full[5],
         full[6],
-        full[7],
         (up_weight, other[1]),
         (down_weight, other[2]),
     )

time: 134 us -> 117 us (0.87)
  Pallas kernels: 125 us -> 109 us
    pallas_call x1, Pallas kernels: 58 us -> 48.2 us  [module(): pl.pallas_call(module_kernel, out_shape=[jax.ShapeDtypeStruct(rows, BF),...]
    pallas_call x1, Pallas kernels: 29.8 us -> 25.2 us  [subsample(): pl.pallas_call(subsample_kernel, out_shape=jax.ShapeDtypeStruct((ROWS, D)...]
    broadcast_in_dim x2 -> x0, local copies, waits for them, and re-layouts: 2.52 us -> none  [the longest x1 1.26 us: local(): norm_gain[None]]
    pallas_call x1, Pallas kernels: 37.2 us -> 35.6 us  [exchange(): pl.pallas_call(exchange_kernel, out_shape=shapes, in_specs=[VMEM_SPEC] *...]
    another operation x0 -> x2, local copies, waits for them, and re-layouts: none -> 1.36 us  [local(): jnp.stack([norm_gain, conv_gain])]
where the time goes in v4:
time: 117 us; the launch traced here: 116 us
  Pallas kernels  109 us (93%)
  local copies, waits for them, and re-layouts  6.08 us (5%)
    pallas_call x1, Pallas kernels, module(): pl.pallas_call(module_kernel, out_shape=[jax.ShapeDtypeStruct(rows, BF),...  48.2 us
    pallas_call x1, Pallas kernels, exchange(): pl.pallas_call(exchange_kernel, out_shape=shapes, in_specs=[VMEM_SPEC] *...  35.6 us
    pallas_call x1, Pallas kernels, subsample(): pl.pallas_call(subsample_kernel, out_shape=jax.ShapeDtypeStruct((ROWS, D)...  25.2 us
    unnamed x7, local copies, waits for them, and re-layouts  4.71 us

profile of v4, /device:TPU:0, one launch (start us, length us, event | category | flops | bytes accessed | tf_op | source)
XLA Modules:
  0.0 116.4 jit_solution(12634382326015862067)
XLA Ops:
  0.6 0.7 stack.9
  1.3 0.7 stack.10
  2.0 0.6 pad_maximum_fusion.refs_8_
  2.6 35.6 %exchange.1 = (bf16[2048,256]{1,0:T(8,128)(2,1)}, f32[512,128]{1,0:T(8,128)}, bf16[256,10240]{1,0:T(8,128)(2,1)}, bf16[9,256]{1,0:T(8,128)(2,1)}, bf16[9,256]{1,...) custom-call(s32[1,64]{1,0:T(1,128)} %bitcast.2, ...), custom_call_target="tpu_custom_call" | custom-call | tf_op jit(solution)/shard_map/exchange/pallas_call | solution.py:199
  38.2 25.2 %subsample.1.features = bf16[512,1024]{1,0:T(8,128)(2,1)} custom-call(bf16[2048,256]{1,0:T(8,128)(2,1)} %get-tuple-element.15.windows, bf16[256,10240]{1,0:T(8,128)(2,1)} %get-tuple-element.16.band_in, bf16[9,256]{1,0:T(8,128)(2,1)} %get-tuple-element.17.depth_a, bf16[256,256]{1,0:T(8,128)(2,1)} %get-tuple-element.18.point_a, ...), custom_call_target="tpu_custom_call" | custom-call | tf_op jit(solution)/shard_map/subsample/pallas_call | solution.py:331
  63.4 48.2 %module.1 = (bf16[512,1024]{1,0:T(8,128)(2,1)}, bf16[512,1024]{1,0:T(8,128)(2,1)}, f32[512,1024]{1,0:T(8,128)}) custom-call(bf16[512,1024]{1,0:T(8,128)(2,1)} %subsample.1.features, f32[512,128]{1,0:T(8,128)} %get-tuple-element.22.keep, bf16[512,1024]{1,0:T(8,128)(2,1)} %cotangent.1, bf16[2,1024]{1,0:T(2,128)(2,1)} %get-tuple-element.23.gains, ...), custom_call_target="tpu_custom_call" | custom-call | tf_op jit(solution)/shard_map/module/pallas_call | solution.py:704
  111.6 0.0 copy-start.1
  111.6 0.0 copy-start
  111.6 2.4 %copy.21 = bf16[512,1024]{1,0:T(8,128)(2,1)} copy(bf16[512,1024]{1,0:T(8,128)(2,1)} %get-tuple-element.30) | data formatting | bytes 2097152
  114.1 0.0 copy-done.1
  114.1 1.0 copy.22
  115.0 0.0 copy-done
  115.0 1.3 %copy.23 = f32[512,1024]{1,0:T(8,128)} copy(f32[512,1024]{1,0:T(8,128)S(1)} %copy-done) | data formatting | bytes 4194304
Async XLA Ops:
  111.6 2.4 %copy-start.1 = (bf16[512,1024]{1,0:T(8,128)(2,1)S(1)}, bf16[512,1024]{1,0:T(8,128)(2,1)}, u32[]{:S(2)}) copy-start(bf16[512,1024]{1,0:T(8,128)(2,1)} %get-tuple-element.31) | copy-start | bytes 3145732
  111.6 3.4 %copy-start = (f32[512,1024]{1,0:T(8,128)S(1)}, f32[512,1024]{1,0:T(8,128)}, u32[]{:S(2)}) copy-start(f32[512,1024]{1,0:T(8,128)} %get-tuple-element.32) | copy-start | bytes 6291460

commit v5 on v4

--- a/solution.py
+++ b/solution.py
@@ -35,11 +35,21 @@
     return jnp.dot(a, b, preferred_element_type=F32)
 
 
-def shifted_peer(me, step):
-    x = (me + step) % 4
-    y = (me // 4 + step // 4) % 4
-    z = (me // 16 + step // 16) % 4
-    return z * 16 + y * 4 + x
+def shifts(me):
+    return tuple([(me // by + k) % 4 for k in range(4)] for by in (1, 4, 16))
+
+
+def peer_at(moved, step):
+    x, y, z = moved
+    return z[step // 16] * 16 + y[step // 4 % 4] * 4 + x[step % 4]
+
+
+def greet_peers(barrier, me, core, moved, steps):
+    pl.semaphore_signal(barrier, inc=1, device_id=(me, 1 - core), device_id_type=MESH)
+    for step in steps:
+        pl.semaphore_signal(
+            barrier, inc=1, device_id=(peer_at(moved, step), core), device_id_type=MESH
+        )
 
 
 N_SMALL = 7
@@ -47,33 +57,29 @@
 
 
 def exchange_kernel(*refs):
-    frames, target, mel = refs[:3]
+    frames, target, mel_in = refs[:3]
     small = refs[3 : 3 + N_SMALL]
     big = refs[10:13]
     windows, keep_out, band_out = refs[13:16]
     small_full = refs[16 : 16 + N_SMALL]
     big_other = refs[23:26]
-    flat, outgoing, incoming, band_in = refs[26:30]
-    small_other = refs[30 : 30 + N_SMALL]
-    small_send, small_recv, big_send, big_recv, send_sem, recv_sem, band_sem = refs[37:]
+    flat, outgoing, incoming, band_in, mel = refs[26:31]
+    small_other = refs[31 : 31 + N_SMALL]
+    small_send, small_recv, big_send, big_recv, send_sem, recv_sem, band_sem, mel_sem = refs[38:]
 
     me = lax.axis_index("dp")
     core = lax.axis_index("fsdp")
     other = 1 - core
     barrier = pltpu.get_barrier_semaphore()
-    pl.semaphore_signal(barrier, inc=1, device_id=(me, other), device_id_type=MESH)
-
-    def greet(step, carry):
-        pl.semaphore_signal(
-            barrier, inc=1, device_id=(shifted_peer(me, step), core), device_id_type=MESH
-        )
-        return carry
-
-    lax.fori_loop(1, N_DP, greet, 0)
+    mel_copy = pltpu.make_async_copy(mel_in, mel, mel_sem)
+    mel_copy.start()
+    moved = shifts(me)
+    greet_peers(barrier, me, core, moved, range(1, N_DP))
 
     picks = (target[...] == iota((N_DP, 64), 0)) & (frames[...] > 0)
     length = jnp.sum(jnp.where(picks, frames[...], 0), axis=1, keepdims=True)
     chosen = jnp.where(picks, 1.0, 0.0).astype(BF)
+    mel_copy.wait()
     for g in range(SPAN):
         rows = dot(chosen, mel[:, g * GROUP : (g + 1) * GROUP])
         rows = jnp.where(length > 8 * g, rows, MARK)
@@ -97,18 +103,16 @@
         copy.start()
         partner.append(copy)
 
-    def send(step, carry):
+    for step in range(1, N_DP):
+        peer = peer_at(moved, step)
         pltpu.make_async_remote_copy(
-            src_ref=outgoing.at[shifted_peer(me, step)],
+            src_ref=outgoing.at[peer],
             dst_ref=incoming.at[me],
             send_sem=send_sem,
             recv_sem=recv_sem,
-            device_id=(shifted_peer(me, step), core),
+            device_id=(peer, core),
             device_id_type=MESH,
         ).start()
-        return carry
-
-    lax.fori_loop(1, N_DP, send, 0)
     for k in range(N_BIG):
         copy = pltpu.make_async_remote_copy(
             src_ref=big[k],
@@ -199,18 +203,20 @@
     out = pl.pallas_call(
         exchange_kernel,
         out_shape=shapes,
-        in_specs=[VMEM_SPEC] * (3 + N_SMALL) + [ANY_SPEC] * N_BIG,
+        in_specs=[VMEM_SPEC] * 2 + [ANY_SPEC] + [VMEM_SPEC] * N_SMALL + [ANY_SPEC] * N_BIG,
         out_specs=[VMEM_SPEC] * 2 + [ANY_SPEC] + [VMEM_SPEC] * N_SMALL + [ANY_SPEC] * N_BIG,
         scratch_shapes=[
             pltpu.VMEM((GROUP // 128, N_DP * SPAN, 128), F32),
             pltpu.VMEM((N_DP, SPAN, GROUP), BF),
             pltpu.VMEM((N_DP, SPAN, GROUP), BF),
             pltpu.VMEM((256, MELS // 2 * CH), BF),
+            pltpu.VMEM((64, SPAN * GROUP), BF),
             *[pltpu.VMEM(a.shape, BF) for a in small],
             pltpu.SemaphoreType.DMA((N_SMALL,)),
             pltpu.SemaphoreType.DMA((N_SMALL,)),
             pltpu.SemaphoreType.DMA((N_BIG,)),
             pltpu.SemaphoreType.DMA((N_BIG,)),
+            pltpu.SemaphoreType.DMA,
             pltpu.SemaphoreType.DMA,
             pltpu.SemaphoreType.DMA,
             pltpu.SemaphoreType.DMA,
@@ -367,6 +373,8 @@
 
 
 def lane_tile(n, start=0):
+    if isinstance(n, int):
+        return pl.ds(start + n * N_TILE, N_TILE)
     return pl.ds(pl.multiple_of(start + n * N_TILE, N_TILE), N_TILE)
 
 
@@ -375,21 +383,12 @@
 OWN = 8
 
 
-def line_of(me, c):
-    x, y, z = me % 4, me // 4 % 4, me // 16
-    return ((x, z * 4 + y), (y, z * 4 + x), (z, y * 4 + x))[c]
-
-
-def device_at(c, a, p):
-    if c == 0:
-        return p // 4 * 16 + p % 4 * 4 + a
-    if c == 1:
-        return p // 4 * 16 + a * 4 + p % 4
-    return a * 16 + p
-
-
-def plane_shift(p, step):
-    return (p // 4 + step // 4) % 4 * 4 + (p + step) % 4
+def placed_at(moved, c, line, plane):
+    steps = [(plane // 4, plane % 4)[k] for k in range(2)]
+    steps.insert((2, 1, 0)[c], line)
+    z, y, x = (moved[2 - k][steps[k]] for k in range(3))
+    place = ((x, z * 4 + y), (y, z * 4 + x), (z, y * 4 + x))[c]
+    return (z * 16 + y * 4 + x, *place)
 
 
 def module_kernel(
@@ -399,22 +398,16 @@
     up, down, normed, stats, gate_a, gate_b, gated, standard_two, slope, hidden, back_out,
     grad_own, to_partner, from_partner, part, shared, big, back_depth, back_proj,
     line_a, line_b, line_c, mid_a, mid_b, mid_c, wide_a, wide_b, wide_c,
-    plane_a, plane_b, plane_c, mine_a, mine_b, mine_c,
+    plane_a, plane_b, plane_c, mine_a, mine_b, mine_c, taps,
     load_sems, partner_send, partner_recv, send_sems, recv_sems, own_sems,
 ):
     me = lax.axis_index("dp")
     core = lax.axis_index("fsdp")
     other = 1 - core
     barrier = pltpu.get_barrier_semaphore()
-    pl.semaphore_signal(barrier, inc=1, device_id=(me, other), device_id_type=MESH)
-
-    def greet(step, carry):
-        pl.semaphore_signal(
-            barrier, inc=1, device_id=(shifted_peer(me, step), core), device_id_type=MESH
-        )
-        return carry
-
-    lax.fori_loop(1, N_DP, greet, 0)
+    moved = shifts(me)
+    near = [k for k in range(1, N_DP) if k < 16 or k % 16 < 4 or k % 4 == 0]
+    greet_peers(barrier, me, core, moved, near)
 
     def part_of(which, width):
         return pl.ds(pl.multiple_of(which * width, width), width)
@@ -454,8 +447,6 @@
     in_row = iota((ROWS, ROWS), 1)
     to_groups = jnp.where(in_row == (out_row % U_DEV) * SPAN + out_row // U_DEV, 1.0, 0.0)
     to_groups = to_groups.astype(BF)
-    to_panels = jnp.where(in_row == (out_row % SPAN) * U_DEV + out_row // SPAN, 1.0, 0.0)
-    to_panels = to_panels.astype(BF)
 
     loads[0].wait()
     loads[1].wait()
@@ -471,13 +462,17 @@
         back_out[:, lane_tile(n)] = jnp.where(keep[:, :1] > 0, moved, 0.0).astype(BF)
         return carry
 
-    lax.fori_loop(0, D // N_TILE, project, 0)
+    for n in range(D // N_TILE):
+        project(n, 0)
+
+    for k in range(KER):
+        taps[k] = jnp.broadcast_to(depth_kernel[k : k + 1], (U_DEV, D))
 
     def conv_rows(g, carry):
         summed = None
-        for k in range(KER):
-            tap = depth_kernel[k : k + 1].astype(F32)
-            term = gated[rows_of(g, k)].astype(F32) * tap
+        for k in range(0, KER, 3):
+            terms = [gated[rows_of(g, k + i)] * taps[k + i] for i in range(3)]
+            term = (terms[0] + terms[1] + terms[2]).astype(F32)
             summed = term if summed is None else summed + term
         centred = summed - row_mean(summed)
         scale = lax.rsqrt(row_mean(centred * centred) + EPSILON)
@@ -493,16 +488,11 @@
 
     lax.fori_loop(0, SPAN, conv_rows, 0)
 
-    def grad_rows(which, n):
-        mine_rows = hidden[:, part_of(which, HALF_D)]
-        return dot_rows(mine_rows, back_out[:, lane_tile(n)])
-
-    def partner_grad(n, carry):
-        to_partner[:, lane_tile(n)] = grad_rows(other, n).astype(BF)
-        return carry
-
-    lax.fori_loop(0, D // N_TILE, partner_grad, 0)
-    pl.semaphore_wait(barrier, N_DP)
+    def grad_rows(which):
+        return dot_rows(hidden[:, part_of(which, HALF_D)], back_out[...])
+
+    to_partner[...] = grad_rows(other).astype(BF)
+    pl.semaphore_wait(barrier, 1 + len(near))
     swap = pltpu.make_async_remote_copy(
         src_ref=to_partner,
         dst_ref=from_partner,
@@ -513,11 +503,7 @@
     )
     swap.start()
 
-    def own_grad(n, carry):
-        grad_own[:, lane_tile(n)] = grad_rows(core, n)
-        return carry
-
-    lax.fori_loop(0, D // N_TILE, own_grad, 0)
+    grad_own[...] = grad_rows(core)
     loads[2].wait()
     loads[3].wait()
     swap.wait()
@@ -556,66 +542,56 @@
 
     def reduce_lines():
         for c, (at, width) in enumerate(LANES):
-            a, p = line_of(me, c)
             for step in range(1, 4):
-                to = (a + step) % 4
+                peer, a, _ = placed_at(moved, c, step, 0)
                 push(
-                    0, c, part.at[line_rows(to), at : at + width], line_in[c].at[step - 1],
-                    device_at(c, to, p),
+                    0, c, part.at[line_rows(a), at : at + width], line_in[c].at[step - 1], peer
                 )
 
     def reduce_planes():
         for c, (at, width) in enumerate(LANES):
-            a, p = line_of(me, c)
+            _, a, _ = placed_at(moved, c, 0, 0)
             await_block(line_in[c], recv_sems.at[0, c])
             total = part[line_rows(a), at : at + width].astype(F32)
             for k in range(3):
                 total = total + line_in[c][k].astype(F32)
             wide[c][...] = total
             mid[c][...] = total.astype(BF)
-        for c, (at, width) in enumerate(LANES):
-            a, p = line_of(me, c)
-
-            def send(step, carry, c=c, a=a, p=p):
-                to = plane_shift(p, step)
-                push(
-                    1, c, mid[c].at[pl.ds(pl.multiple_of(to * OWN, OWN), OWN)],
-                    plane_in[c].at[step - 1], device_at(c, a, to),
-                )
-                return carry
-
-            lax.fori_loop(1, 16, send, 0)
+        for c in range(3):
+            for step in range(1, 16):
+                peer, _, p = placed_at(moved, c, 0, step)
+                rows = pl.ds(pl.multiple_of(p * OWN, OWN), OWN)
+                push(1, c, mid[c].at[rows], plane_in[c].at[step - 1], peer)
+
+    def spot_of(c):
+        at, width = LANES[c]
+        _, a, p = placed_at(moved, c, 0, 0)
+        return shared.at[own_rows(a, p), at : at + width]
 
     def gather_planes():
-        for c, (at, width) in enumerate(LANES):
-            a, p = line_of(me, c)
+        for c in range(3):
+            _, _, p = placed_at(moved, c, 0, 0)
             await_block(plane_in[c], recv_sems.at[1, c])
             total = wide[c][pl.ds(pl.multiple_of(p * OWN, OWN), OWN)]
             for k in range(15):
                 total = total + plane_in[c][k].astype(F32)
             mine[c][...] = (total * (1.0 / math.sqrt(ROWS * N_DP * 2))).astype(BF)
-        for c, (at, width) in enumerate(LANES):
-            a, p = line_of(me, c)
-            spot = shared.at[own_rows(a, p), at : at + width]
-            pltpu.make_async_copy(mine[c], spot, own_sems.at[c]).start()
-
-            def send(step, carry, c=c, a=a, p=p, spot=spot):
-                push(2, c, mine[c], spot, device_at(c, a, plane_shift(p, step)))
-                return carry
-
-            lax.fori_loop(1, 16, send, 0)
+        for c in range(3):
+            pltpu.make_async_copy(mine[c], spot_of(c), own_sems.at[c]).start()
+            for step in range(1, 16):
+                push(2, c, mine[c], spot_of(c), placed_at(moved, c, 0, step)[0])
 
     def gather_lines():
         for c, (at, width) in enumerate(LANES):
-            a, p = line_of(me, c)
-            spot = shared.at[own_rows(a, p), at : at + width]
-            pltpu.make_async_copy(mine[c], spot, own_sems.at[c]).wait()
+            pltpu.make_async_copy(mine[c], spot_of(c), own_sems.at[c]).wait()
             await_block(plane_in[c], recv_sems.at[2, c])
-            block = shared.at[line_rows(a), at : at + width]
+            block = shared.at[line_rows(placed_at(moved, c, 0, 0)[1]), at : at + width]
             for step in range(1, 4):
-                push(3, c, block, block, device_at(c, (a + step) % 4, p))
+                push(3, c, block, block, placed_at(moved, c, step, 0)[0])
 
     reduce_lines()
+    to_panels = jnp.where(in_row == (out_row % SPAN) * U_DEV + out_row // SPAN, 1.0, 0.0)
+    to_panels = to_panels.astype(BF)
 
     def output(n, carry):
         mixed = dot(hidden[...], down[:, lane_tile(n)])
@@ -735,6 +711,7 @@
             *[pltpu.VMEM((LINE, width), F32) for _, width in LANES],
             *[pltpu.VMEM((15, OWN, width), BF) for _, width in LANES],
             *[pltpu.VMEM((OWN, width), BF) for _, width in LANES],
+            pltpu.VMEM((KER, U_DEV, D), BF),
             pltpu.SemaphoreType.DMA((4,)),
             pltpu.SemaphoreType.DMA,
             pltpu.SemaphoreType.DMA,

time: 117 us -> 110 us (0.940)
  Pallas kernels: 109 us -> 103 us
    pallas_call x1, Pallas kernels: 48.2 us -> 43.3 us  [module(): pl.pallas_call(module_kernel, out_shape=[jax.ShapeDtypeStruct(rows, BF),...]
    pallas_call x1, Pallas kernels: 35.6 us -> 34 us  [exchange(): pl.pallas_call(exchange_kernel, out_shape=shapes, in_specs=[VMEM_SPEC] *...]
where the time goes in v5:
time: 110 us
  Pallas kernels  103 us (94%)
  local copies, waits for them, and re-layouts  6.08 us (6%)
    pallas_call x1, Pallas kernels, module(): pl.pallas_call(module_kernel, out_shape=[jax.ShapeDtypeStruct(rows, BF),...  43.3 us
    pallas_call x1, Pallas kernels, exchange(): pl.pallas_call(exchange_kernel, out_shape=shapes, in_specs=[VMEM_SPEC] *...  34 us
    pallas_call x1, Pallas kernels, subsample(): pl.pallas_call(subsample_kernel, out_shape=jax.ShapeDtypeStruct((ROWS, D)...  25.2 us
    unnamed x7, local copies, waits for them, and re-layouts  4.71 us

profile of v5, /device:TPU:0, one launch (start us, length us, event | category | flops | bytes accessed | tf_op | source)
XLA Modules:
  0.0 109.9 jit_solution(637026314515219978)
XLA Ops:
  0.6 0.7 stack.9
  1.3 0.7 stack.10
  2.0 0.6 pad_maximum_fusion.refs_8_
  2.6 34.0 %exchange.1 = (bf16[2048,256]{1,0:T(8,128)(2,1)}, f32[512,128]{1,0:T(8,128)}, bf16[256,10240]{1,0:T(8,128)(2,1)}, bf16[9,256]{1,0:T(8,128)(2,1)}, bf16[9,256]{1,...) custom-call(s32[1,64]{1,0:T(1,128)} %bitcast.2, ...), custom_call_target="tpu_custom_call" | custom-call | tf_op jit(solution)/shard_map/exchange/pallas_call | solution.py:203
  36.6 25.2 %subsample.1.features = bf16[512,1024]{1,0:T(8,128)(2,1)} custom-call(bf16[2048,256]{1,0:T(8,128)(2,1)} %get-tuple-element.15.windows, bf16[256,10240]{1,0:T(8,128)(2,1)} %get-tuple-element.16.band_in, bf16[9,256]{1,0:T(8,128)(2,1)} %get-tuple-element.17.depth_a, bf16[256,256]{1,0:T(8,128)(2,1)} %get-tuple-element.18.point_a, ...), custom_call_target="tpu_custom_call" | custom-call | tf_op jit(solution)/shard_map/subsample/pallas_call | solution.py:337
  61.9 43.3 %module.1 = (bf16[512,1024]{1,0:T(8,128)(2,1)}, bf16[512,1024]{1,0:T(8,128)(2,1)}, f32[512,1024]{1,0:T(8,128)}) custom-call(bf16[512,1024]{1,0:T(8,128)(2,1)} %subsample.1.features, f32[512,128]{1,0:T(8,128)} %get-tuple-element.22.keep, bf16[512,1024]{1,0:T(8,128)(2,1)} %cotangent.1, bf16[2,1024]{1,0:T(2,128)(2,1)} %get-tuple-element.23.gains, ...), custom_call_target="tpu_custom_call" | custom-call | tf_op jit(solution)/shard_map/module/pallas_call | solution.py:680
  105.2 0.0 copy-start.1
  105.2 0.0 copy-start
  105.2 2.4 %copy.21 = bf16[512,1024]{1,0:T(8,128)(2,1)} copy(bf16[512,1024]{1,0:T(8,128)(2,1)} %get-tuple-element.30) | data formatting | bytes 2097152
  107.6 0.0 copy-done.1
  107.6 1.0 copy.22
  108.6 0.0 copy-done
  108.6 1.3 %copy.23 = f32[512,1024]{1,0:T(8,128)} copy(f32[512,1024]{1,0:T(8,128)S(1)} %copy-done) | data formatting | bytes 4194304
Async XLA Ops:
  105.2 2.4 %copy-start.1 = (bf16[512,1024]{1,0:T(8,128)(2,1)S(1)}, bf16[512,1024]{1,0:T(8,128)(2,1)}, u32[]{:S(2)}) copy-start(bf16[512,1024]{1,0:T(8,128)(2,1)} %get-tuple-element.31) | copy-start | bytes 3145732
  105.2 3.4 %copy-start = (f32[512,1024]{1,0:T(8,128)S(1)}, f32[512,1024]{1,0:T(8,128)}, u32[]{:S(2)}) copy-start(f32[512,1024]{1,0:T(8,128)} %get-tuple-element.32) | copy-start | bytes 6291460

commit v6 on v5

--- a/solution.py
+++ b/solution.py
@@ -52,20 +52,21 @@
         )
 
 
-N_SMALL = 7
+N_SMALL = 8
+GAINS = (5, 6)
 N_BIG = 3
 
 
 def exchange_kernel(*refs):
     frames, target, mel_in = refs[:3]
     small = refs[3 : 3 + N_SMALL]
-    big = refs[10:13]
-    windows, keep_out, band_out = refs[13:16]
-    small_full = refs[16 : 16 + N_SMALL]
-    big_other = refs[23:26]
-    flat, outgoing, incoming, band_in, mel = refs[26:31]
-    small_other = refs[31 : 31 + N_SMALL]
-    small_send, small_recv, big_send, big_recv, send_sem, recv_sem, band_sem, mel_sem = refs[38:]
+    big = refs[11:14]
+    windows, keep_out, band_out = refs[14:17]
+    small_full = refs[17 : 17 + N_SMALL]
+    big_other = refs[25:28]
+    flat, outgoing, incoming, band_in, mel = refs[28:33]
+    small_other = refs[33 : 33 + N_SMALL]
+    small_send, small_recv, big_send, big_recv, send_sem, recv_sem, band_sem, mel_sem = refs[41:]
 
     me = lax.axis_index("dp")
     core = lax.axis_index("fsdp")
@@ -128,9 +129,15 @@
 
     for k in range(N_SMALL):
         partner[k].wait()
-        width = small[k].shape[1]
-        small_full[k][:, pl.ds(pl.multiple_of(core * width, 128), width)] = small[k][...]
-        small_full[k][:, pl.ds(pl.multiple_of(other * width, 128), width)] = small_other[k][...]
+        for which, ref in ((core, small[k]), (other, small_other[k])):
+            if k in GAINS:
+                lines = ref[...].astype(F32)
+                for i in range(D // 2 // 128):
+                    at = pl.multiple_of(which * (D // 2) + i * 128, 128)
+                    small_full[k][:, pl.ds(at, 128)] = lines[i : i + 1].astype(BF)
+            else:
+                width = ref.shape[1]
+                small_full[k][:, pl.ds(pl.multiple_of(which * width, 128), width)] = ref[...]
 
     taps = small_full[0][...]
     row = iota((256, 9), 0)
@@ -192,7 +199,10 @@
 
 
 def exchange(frames, target, mel, small, big):
-    small_full = [jax.ShapeDtypeStruct((a.shape[0], 2 * a.shape[1]), BF) for a in small]
+    small_full = [
+        jax.ShapeDtypeStruct((1, D) if k in GAINS else (a.shape[0], 2 * a.shape[1]), BF)
+        for k, a in enumerate(small)
+    ]
     shapes = [
         jax.ShapeDtypeStruct((4 * ROWS, 256), BF),
         jax.ShapeDtypeStruct((ROWS, 128), F32),
@@ -392,11 +402,11 @@
 
 
 def module_kernel(
-    features, keep, cotangent, gains, depth_kernel,
+    features, keep, cotangent, norm_gain, conv_gain, depth_kernel,
     up_own, up_other, down_own, down_other,
-    layer_out, grad_input, grad_down,
+    layer_out, grad_input, shared,
     up, down, normed, stats, gate_a, gate_b, gated, standard_two, slope, hidden, back_out,
-    grad_own, to_partner, from_partner, part, shared, big, back_depth, back_proj,
+    grad_own, to_partner, from_partner, part, big, back_depth, back_proj,
     line_a, line_b, line_c, mid_a, mid_b, mid_c, wide_a, wide_b, wide_c,
     plane_a, plane_b, plane_c, mine_a, mine_b, mine_c, taps,
     load_sems, partner_send, partner_recv, send_sems, recv_sems, own_sems,
@@ -424,8 +434,8 @@
     def rows_of(g, shift=0):
         return pl.ds(pl.multiple_of((g + shift) * U_DEV, U_DEV), U_DEV)
 
-    gain_one = gains[0:1].astype(F32)
-    gain_two = gains[1:2].astype(F32)
+    gain_one = norm_gain[...].astype(F32)
+    gain_two = conv_gain[...].astype(F32)
 
     def norm_rows(g, carry):
         values = features[rows_of(g)].astype(F32)
@@ -493,27 +503,19 @@
 
     to_partner[...] = grad_rows(other).astype(BF)
     pl.semaphore_wait(barrier, 1 + len(near))
-    swap = pltpu.make_async_remote_copy(
-        src_ref=to_partner,
-        dst_ref=from_partner,
-        send_sem=partner_send,
-        recv_sem=partner_recv,
-        device_id=(me, other),
-        device_id_type=MESH,
-    )
-    swap.start()
-
+    swaps = []
+    for c, (at, width) in enumerate(LANES):
+        copy = pltpu.make_async_remote_copy(
+            src_ref=to_partner.at[:, at : at + width],
+            dst_ref=from_partner.at[:, at : at + width],
+            send_sem=partner_send.at[c],
+            recv_sem=partner_recv.at[c],
+            device_id=(me, other),
+            device_id_type=MESH,
+        )
+        copy.start()
+        swaps.append(copy)
     grad_own[...] = grad_rows(core)
-    loads[2].wait()
-    loads[3].wait()
-    swap.wait()
-
-    def add_partner(n, carry):
-        rows = pl.ds(pl.multiple_of(n * 64, 64), 64)
-        part[rows] = (grad_own[rows] + from_partner[rows].astype(F32)).astype(BF)
-        return carry
-
-    lax.fori_loop(0, HALF_D // 64, add_partner, 0)
 
     line_in = (line_a, line_b, line_c)
     mid = (mid_a, mid_b, mid_c)
@@ -542,6 +544,9 @@
 
     def reduce_lines():
         for c, (at, width) in enumerate(LANES):
+            swaps[c].wait()
+            lanes = slice(at, at + width)
+            part[:, lanes] = (grad_own[:, lanes] + from_partner[:, lanes].astype(F32)).astype(BF)
             for step in range(1, 4):
                 peer, a, _ = placed_at(moved, c, step, 0)
                 push(
@@ -590,6 +595,8 @@
                 push(3, c, block, block, placed_at(moved, c, step, 0)[0])
 
     reduce_lines()
+    loads[2].wait()
+    loads[3].wait()
     to_panels = jnp.where(in_row == (out_row % SPAN) * U_DEV + out_row // SPAN, 1.0, 0.0)
     to_panels = to_panels.astype(BF)
 
@@ -662,12 +669,6 @@
     for c in range(3):
         await_block(line_in[c], recv_sems.at[3, c])
 
-    def place(n, carry):
-        rows = pl.ds(pl.multiple_of(n * 64, 64), 64)
-        grad_down[rows] = shared[rows].astype(F32)
-        return carry
-
-    lax.fori_loop(0, HALF_D // 64, place, 0)
     for c in range(3):
         await_block(line_in[c], send_sems.at[0, c])
         await_block(plane_in[c], send_sems.at[1, c])
@@ -675,16 +676,16 @@
         await_block(line_in[c], send_sems.at[3, c])
 
 
-def module(features, keep, cotangent, gains, depth_kernel, ups, downs):
+def module(features, keep, cotangent, norm_gain, conv_gain, depth_kernel, ups, downs):
     rows = (ROWS, D)
     return pl.pallas_call(
         module_kernel,
         out_shape=[
             jax.ShapeDtypeStruct(rows, BF),
             jax.ShapeDtypeStruct(rows, BF),
-            jax.ShapeDtypeStruct((HALF_D, D), F32),
+            jax.ShapeDtypeStruct((HALF_D, D), BF),
         ],
-        in_specs=[VMEM_SPEC] * 5 + [ANY_SPEC] * 4,
+        in_specs=[VMEM_SPEC] * 6 + [ANY_SPEC] * 4,
         out_specs=[VMEM_SPEC] * 3,
         scratch_shapes=[
             pltpu.VMEM((D, 2 * D), BF),
@@ -702,7 +703,6 @@
             pltpu.VMEM((HALF_D, D), BF),
             pltpu.VMEM((HALF_D, D), BF),
             pltpu.VMEM((HALF_D, D), BF),
-            pltpu.VMEM((HALF_D, D), BF),
             pltpu.VMEM(rows, F32),
             pltpu.VMEM((ROWS + 2 * BORDER, D), F32),
             pltpu.VMEM((ROWS, 2 * D), BF),
@@ -713,8 +713,8 @@
             *[pltpu.VMEM((OWN, width), BF) for _, width in LANES],
             pltpu.VMEM((KER, U_DEV, D), BF),
             pltpu.SemaphoreType.DMA((4,)),
-            pltpu.SemaphoreType.DMA,
-            pltpu.SemaphoreType.DMA,
+            pltpu.SemaphoreType.DMA((3,)),
+            pltpu.SemaphoreType.DMA((3,)),
             pltpu.SemaphoreType.DMA((4, 3)),
             pltpu.SemaphoreType.DMA((4, 3)),
             pltpu.SemaphoreType.DMA((3,)),
@@ -723,7 +723,30 @@
             collective_id=1, has_side_effects=True, vmem_limit_bytes=67043328
         ),
         name="module",
-    )(features, keep, cotangent, gains, depth_kernel, *ups, *downs)
+    )(features, keep, cotangent, norm_gain, conv_gain, depth_kernel, *ups, *downs)
+
+
+def finish_kernel(layer_in, grad_in, down_in, layer_out, grad_input, grad_down):
+    layer_out[...] = layer_in[...]
+    grad_input[...] = grad_in[...]
+    grad_down[...] = down_in[...].astype(F32)
+
+
+def finish(layer_out, grad_input, grad_down):
+    block = pl.BlockSpec((128, D), lambda i: (i, 0))
+    return pl.pallas_call(
+        finish_kernel,
+        grid=(ROWS // 128,),
+        out_shape=[
+            jax.ShapeDtypeStruct((ROWS, D), BF),
+            jax.ShapeDtypeStruct((ROWS, D), BF),
+            jax.ShapeDtypeStruct((HALF_D, D), F32),
+        ],
+        in_specs=[block] * 3,
+        out_specs=[block] * 3,
+        compiler_params=pltpu.CompilerParams(vmem_limit_bytes=67043328),
+        name="finish",
+    )(layer_out, grad_input, grad_down)
 
 
 def local(
@@ -749,21 +772,24 @@
         point_a,
         depth_b,
         point_b,
-        jnp.stack([norm_gain, conv_gain]),
+        norm_gain.reshape(-1, 128),
+        conv_gain.reshape(-1, 128),
         depth_kernel,
     )
     big = (linear_weight, up_weight, down_weight)
     windows, keep, band, full, other = exchange(frames[None], target[None], mel_panels, small, big)
     features = subsample(windows, band, *full[1:5], linear_weight, other[0])
-    return module(
+    results = module(
         features,
         keep,
         cotangent,
         full[5],
         full[6],
+        full[7],
         (up_weight, other[1]),
         (down_weight, other[2]),
     )
+    return tuple(finish(*results))
 
 
 def solution(mesh):

time: 110 us -> 107 us (0.973)
  local copies, waits for them, and re-layouts: 6.08 us -> 0 us
  Pallas kernels: 103 us -> 106 us
    unnamed x7 -> x0, local copies, waits for them, and re-layouts: 4.71 us -> none
    pallas_call x0 -> x1, Pallas kernels: none -> 4.37 us  [finish(): pl.pallas_call(finish_kernel, grid=(ROWS // 128,), out_shape=[jax.ShapeDt...]
    another operation x2 -> x0, local copies, waits for them, and re-layouts: 1.36 us -> none  [local(): jnp.stack([norm_gain, conv_gain])]
where the time goes in v6:
time: 107 us
  Pallas kernels  106 us (99%)
    pallas_call x1, Pallas kernels, module(): pl.pallas_call(module_kernel, out_shape=[jax.ShapeDtypeStruct(rows, BF),...  42.7 us
    pallas_call x1, Pallas kernels, exchange(): pl.pallas_call(exchange_kernel, out_shape=shapes, in_specs=[VMEM_SPEC] *...  34.1 us
    pallas_call x1, Pallas kernels, subsample(): pl.pallas_call(subsample_kernel, out_shape=jax.ShapeDtypeStruct((ROWS, D)...  25.2 us
    pallas_call x1, Pallas kernels, finish(): pl.pallas_call(finish_kernel, grid=(ROWS // 128,), out_shape=[jax.ShapeDt...  4.37 us

profile of v6, /device:TPU:0, one launch (start us, length us, event | category | flops | bytes accessed | tf_op | source)
XLA Modules:
  0.0 107.1 jit_solution(318501503468706575)
XLA Ops:
  0.6 34.1 %exchange.1 = (bf16[2048,256]{1,0:T(8,128)(2,1)}, f32[512,128]{1,0:T(8,128)}, bf16[256,10240]{1,0:T(8,128)(2,1)}, bf16[9,256]{1,0:T(8,128)(2,1)}, bf16[9,256]{1,...) custom-call(s32[1,64]{1,0:T(1,128)} %bitcast.6, ...), custom_call_target="tpu_custom_call" | custom-call | tf_op jit(solution)/shard_map/exchange/pallas_call | solution.py:213
  34.7 25.2 %subsample.1.features = bf16[512,1024]{1,0:T(8,128)(2,1)} custom-call(bf16[2048,256]{1,0:T(8,128)(2,1)} %get-tuple-element.19.windows, bf16[256,10240]{1,0:T(8,128)(2,1)} %get-tuple-element.20.band_in, bf16[9,256]{1,0:T(8,128)(2,1)} %get-tuple-element.21.depth_a, bf16[256,256]{1,0:T(8,128)(2,1)} %get-tuple-element.22.point_a, ...), custom_call_target="tpu_custom_call" | custom-call | tf_op jit(solution)/shard_map/subsample/pallas_call | solution.py:347
  60.0 42.7 %module.1 = (bf16[512,1024]{1,0:T(8,128)(2,1)}, bf16[512,1024]{1,0:T(8,128)(2,1)}, bf16[512,1024]{1,0:T(8,128)(2,1)}) custom-call(bf16[512,1024]{1,0:T(8,128)(2,1)} %subsample.1.features, f32[512,128]{1,0:T(8,128)} %get-tuple-element.26.keep, bf16[512,1024]{1,0:T(8,128)(2,1)} %cotangent.1, bf16[1,1024]{1,0:T(2,128)(2,1)} %get-tuple-element.27.norm_gain, ...), custom_call_target="tpu_custom_call" | custom-call | tf_op jit(solution)/shard_map/module/pallas_call | solution.py:681
  102.7 4.4 %finish.1 = (bf16[512,1024]{1,0:T(8,128)(2,1)}, bf16[512,1024]{1,0:T(8,128)(2,1)}, f32[512,1024]{1,0:T(8,128)}) custom-call(bf16[512,1024]{1,0:T(8,128)(2,1)} %get-tuple-element.32.layer_in, bf16[512,1024]{1,0:T(8,128)(2,1)} %get-tuple-element.33.grad_in, bf16[512,1024]{1,0:T(8,128)(2,1)} %get-tuple-element.34.down_in), custom_call_target="tpu_custom_call" | custom-call | tf_op jit(solution)/shard_map/finish/pallas_call | solution.py:737

commit v7 on v6

--- a/solution.py
+++ b/solution.py
@@ -39,6 +39,14 @@
     return tuple([(me // by + k) % 4 for k in range(4)] for by in (1, 4, 16))
 
 
+def hops(step):
+    return sum((0, 1, 2, 1)[step // by % 4] for by in (1, 4, 16))
+
+
+FAR_FIRST = sorted(range(1, N_DP), key=lambda step: -hops(step))
+PLANE_STEPS = sorted(range(1, 16), key=lambda step: -hops(step))
+
+
 def peer_at(moved, step):
     x, y, z = moved
     return z[step // 16] * 16 + y[step // 4 % 4] * 4 + x[step % 4]
@@ -104,7 +112,7 @@
         copy.start()
         partner.append(copy)
 
-    for step in range(1, N_DP):
+    for step in FAR_FIRST:
         peer = peer_at(moved, step)
         pltpu.make_async_remote_copy(
             src_ref=outgoing.at[peer],
@@ -405,7 +413,7 @@
     features, keep, cotangent, norm_gain, conv_gain, depth_kernel,
     up_own, up_other, down_own, down_other,
     layer_out, grad_input, shared,
-    up, down, normed, stats, gate_a, gate_b, gated, standard_two, slope, hidden, back_out,
+    up, down, normed, stats, gate_a, gate_b, gated, standard_two, hidden, back_out,
     grad_own, to_partner, from_partner, part, big, back_depth, back_proj,
     line_a, line_b, line_c, mid_a, mid_b, mid_c, wide_a, wide_b, wide_c,
     plane_a, plane_b, plane_c, mine_a, mine_b, mine_c, taps,
@@ -466,7 +474,7 @@
         gate = jax.nn.sigmoid(dot(normed[...], up[:, lane_tile(n, D)]))
         both = value * gate
         gate_a[:, lane_tile(n)] = gate
-        gate_b[:, lane_tile(n)] = both * (1.0 - gate)
+        gate_b[:, lane_tile(n)] = both
         gated[BORDER : BORDER + ROWS, lane_tile(n)] = (keep[:, :1] * both).astype(BF)
         moved = dot(to_groups, cotangent[:, lane_tile(n)])
         back_out[:, lane_tile(n)] = jnp.where(keep[:, :1] > 0, moved, 0.0).astype(BF)
@@ -492,7 +500,6 @@
         act = active * swish
         hidden[rows_of(g)] = act.astype(BF)
         standard_two[rows_of(g)] = standard
-        slope[rows_of(g)] = (swish + act * (1.0 - swish)) * gain_two
         stats[2, rows_of(g)] = jnp.broadcast_to(scale, (U_DEV, 128))
         return carry
 
@@ -563,7 +570,7 @@
             wide[c][...] = total
             mid[c][...] = total.astype(BF)
         for c in range(3):
-            for step in range(1, 16):
+            for step in PLANE_STEPS:
                 peer, _, p = placed_at(moved, c, 0, step)
                 rows = pl.ds(pl.multiple_of(p * OWN, OWN), OWN)
                 push(1, c, mid[c].at[rows], plane_in[c].at[step - 1], peer)
@@ -583,7 +590,7 @@
             mine[c][...] = (total * (1.0 / math.sqrt(ROWS * N_DP * 2))).astype(BF)
         for c in range(3):
             pltpu.make_async_copy(mine[c], spot_of(c), own_sems.at[c]).start()
-            for step in range(1, 16):
+            for step in PLANE_STEPS:
                 push(2, c, mine[c], spot_of(c), placed_at(moved, c, 0, step)[0])
 
     def gather_lines():
@@ -617,8 +624,10 @@
     lax.fori_loop(0, D // N_TILE, back_hidden, 0)
 
     def back_norm(g, carry):
-        error = big[rows_of(g)] * slope[rows_of(g)]
         standard = standard_two[rows_of(g)]
+        active = standard * gain_two
+        swish = jax.nn.sigmoid(active)
+        error = big[rows_of(g)] * ((swish + active * swish * (1.0 - swish)) * gain_two)
         inner = error - row_mean(error) - standard * row_mean(error * standard)
         back_depth[rows_of(g, KER // 2)] = stats[2, rows_of(g), :1] * inner
         return carry
@@ -634,8 +643,10 @@
             term = back_depth[rows_of(g, KER - 1 - k)] * tap
             summed = term if summed is None else summed + term
         summed = keep[rows_of(g), :1] * summed
-        back_proj[rows_of(g), 0:D] = (summed * gate_a[rows_of(g)]).astype(BF)
-        back_proj[rows_of(g), D : 2 * D] = (summed * gate_b[rows_of(g)]).astype(BF)
+        gate = gate_a[rows_of(g)]
+        back_proj[rows_of(g), 0:D] = (summed * gate).astype(BF)
+        inner = summed * gate_b[rows_of(g)] * (1.0 - gate)
+        back_proj[rows_of(g), D : 2 * D] = inner.astype(BF)
         return carry
 
     lax.fori_loop(0, SPAN, back_conv, 0)
@@ -695,7 +706,6 @@
             pltpu.VMEM(rows, F32),
             pltpu.VMEM(rows, F32),
             pltpu.VMEM((ROWS + 2 * BORDER, D), BF),
-            pltpu.VMEM(rows, F32),
             pltpu.VMEM(rows, F32),
             pltpu.VMEM(rows, BF),
             pltpu.VMEM(rows, BF),
@@ -726,24 +736,49 @@
     )(features, keep, cotangent, norm_gain, conv_gain, depth_kernel, *ups, *downs)
 
 
-def finish_kernel(layer_in, grad_in, down_in, layer_out, grad_input, grad_down):
-    layer_out[...] = layer_in[...]
-    grad_input[...] = grad_in[...]
-    grad_down[...] = down_in[...].astype(F32)
+def finish_kernel(
+    layer_in, grad_in, down_in, layer_out, grad_input, grad_down, held, wide, in_sems, out_sems
+):
+    blocks = [slice(k * 128, (k + 1) * 128) for k in range(ROWS // 128)]
+    pairs = ((down_in, grad_down), (layer_in, layer_out), (grad_in, grad_input))
+
+    def arriving(k, n):
+        rows = blocks[n]
+        return pltpu.make_async_copy(pairs[k][0].at[rows], held.at[k, rows], in_sems.at[k, n])
+
+    def leaving(k, n):
+        rows = blocks[n]
+        source = wide.at[rows] if k == 0 else held.at[k, rows]
+        return pltpu.make_async_copy(source, pairs[k][1].at[rows], out_sems.at[k, n])
+
+    order = [(k, n) for n in range(len(blocks)) for k in range(3)]
+    for k, n in order:
+        arriving(k, n).start()
+    for k, n in order:
+        arriving(k, n).wait()
+        if k == 0:
+            wide[blocks[n]] = held[0, blocks[n]].astype(F32)
+        leaving(k, n).start()
+    for k, n in order:
+        leaving(k, n).wait()
 
 
 def finish(layer_out, grad_input, grad_down):
-    block = pl.BlockSpec((128, D), lambda i: (i, 0))
     return pl.pallas_call(
         finish_kernel,
-        grid=(ROWS // 128,),
         out_shape=[
             jax.ShapeDtypeStruct((ROWS, D), BF),
             jax.ShapeDtypeStruct((ROWS, D), BF),
             jax.ShapeDtypeStruct((HALF_D, D), F32),
         ],
-        in_specs=[block] * 3,
-        out_specs=[block] * 3,
+        in_specs=[ANY_SPEC] * 3,
+        out_specs=[ANY_SPEC] * 3,
+        scratch_shapes=[
+            pltpu.VMEM((3, ROWS, D), BF),
+            pltpu.VMEM((HALF_D, D), F32),
+            pltpu.SemaphoreType.DMA((3, 4)),
+            pltpu.SemaphoreType.DMA((3, 4)),
+        ],
         compiler_params=pltpu.CompilerParams(vmem_limit_bytes=67043328),
         name="finish",
     )(layer_out, grad_input, grad_down)

time: 107 us -> 103 us (0.963)
  Pallas kernels: 106 us -> 102 us
    pallas_call x1, Pallas kernels: 34.1 us -> 30.1 us  [exchange(): pl.pallas_call(exchange_kernel, out_shape=shapes, in_specs=[VMEM_SPEC] *...]
    pallas_call x1, Pallas kernels: 4.37 us -> 3.19 us  [finish(): pl.pallas_call(finish_kernel, out_shape=[jax.ShapeDtypeStruct((ROWS, D),...]
where the time goes in v7:
time: 103 us; the launch traced here: 102 us
  Pallas kernels  102 us (99%)
    pallas_call x1, Pallas kernels, module(): pl.pallas_call(module_kernel, out_shape=[jax.ShapeDtypeStruct(rows, BF),...  43.1 us
    pallas_call x1, Pallas kernels, exchange(): pl.pallas_call(exchange_kernel, out_shape=shapes, in_specs=[VMEM_SPEC] *...  30.1 us
    pallas_call x1, Pallas kernels, subsample(): pl.pallas_call(subsample_kernel, out_shape=jax.ShapeDtypeStruct((ROWS, D)...  25.2 us
    pallas_call x1, Pallas kernels, finish(): pl.pallas_call(finish_kernel, out_shape=[jax.ShapeDtypeStruct((ROWS, D),...  3.19 us

profile of v7, /device:TPU:0, one launch (start us, length us, event | category | flops | bytes accessed | tf_op | source)
XLA Modules:
  0.0 102.5 jit_solution(7260094207517218276)
XLA Ops:
  0.6 30.1 %exchange.1 = (bf16[2048,256]{1,0:T(8,128)(2,1)}, f32[512,128]{1,0:T(8,128)}, bf16[256,10240]{1,0:T(8,128)(2,1)}, bf16[9,256]{1,0:T(8,128)(2,1)}, bf16[9,256]{1,...) custom-call(s32[1,64]{1,0:T(1,128)} %bitcast.6, ...), custom_call_target="tpu_custom_call" | custom-call | tf_op jit(solution)/shard_map/exchange/pallas_call | solution.py:221
  30.8 25.2 %subsample.1.features = bf16[512,1024]{1,0:T(8,128)(2,1)} custom-call(bf16[2048,256]{1,0:T(8,128)(2,1)} %get-tuple-element.19.windows, bf16[256,10240]{1,0:T(8,128)(2,1)} %get-tuple-element.20.band_in, bf16[9,256]{1,0:T(8,128)(2,1)} %get-tuple-element.21.depth_a, bf16[256,256]{1,0:T(8,128)(2,1)} %get-tuple-element.22.point_a, ...), custom_call_target="tpu_custom_call" | custom-call | tf_op jit(solution)/shard_map/subsample/pallas_call | solution.py:355
  56.0 43.1 %module.1 = (bf16[512,1024]{1,0:T(8,128)(2,1)}, bf16[512,1024]{1,0:T(8,128)(2,1)}, bf16[512,1024]{1,0:T(8,128)(2,1)}) custom-call(bf16[512,1024]{1,0:T(8,128)(2,1)} %subsample.1.features, f32[512,128]{1,0:T(8,128)} %get-tuple-element.26.keep, bf16[512,1024]{1,0:T(8,128)(2,1)} %cotangent.1, bf16[1,1024]{1,0:T(2,128)(2,1)} %get-tuple-element.27.norm_gain, ...), custom_call_target="tpu_custom_call" | custom-call | tf_op jit(solution)/shard_map/module/pallas_call | solution.py:692
  99.1 3.2 %finish.1 = (bf16[512,1024]{1,0:T(8,128)(2,1)}, bf16[512,1024]{1,0:T(8,128)(2,1)}, f32[512,1024]{1,0:T(8,128)}) custom-call(bf16[512,1024]{1,0:T(8,128)(2,1)} %get-tuple-element.32.layer_in, bf16[512,1024]{1,0:T(8,128)(2,1)} %get-tuple-element.33.grad_in, bf16[512,1024]{1,0:T(8,128)(2,1)} %get-tuple-element.34.down_in), custom_call_target="tpu_custom_call" | custom-call | tf_op jit(solution)/shard_map/finish/pallas_call | solution.py:767
